TPU v7x, 256 devices: a whole 4x4x8 slice. The times are simulated.
256 devices in a mesh: rep: 2 (over core), seq: 16 (over z, y_hi), head: 8 (over y_lo, x).
Axes of the slice: x: 4, y: 4 (y_hi: 2, y_lo: 2; y = y_hi * 2 + y_lo), z: 8, core: 2. Of those that a mesh axis runs over, the one named last changes fastest.
Arguments:
- query_latent: bfloat16 [2, 2048, 1536], P('rep', 'seq'), may hold values from -72 to 72
- kv_latent: bfloat16 [2, 2048, 576], P('rep', 'seq'), may hold values from -72 to 72
- query_up: bfloat16 [1536, 12288], P(None, 'head'), may hold values from -0.15625 to 0.15625
- kv_up: bfloat16 [512, 16384], P(None, 'head'), may hold values from -0.25 to 0.25
- out_grad: bfloat16 [2, 2048, 8192], P('rep', 'seq', 'head'), may hold values from -6 to 6
- positions: int32 [2, 2048], P('rep'), may hold values from 0 to 1535, as said below
Outputs:
- query_grad: bfloat16 [2, 2048, 1536], P('rep', 'seq')
- latent_grad: bfloat16 [2, 2048, 576], P('rep', ('seq', 'head'))
- query_up_grad: bfloat16 [1536, 12288], P(('rep', 'seq'), 'head')
Inputs may be any that keep to these rules, and one draw needn't show every extreme that they name: In each window, positions count tokens from the start of their document, rising by one a token and restarting at 0 where a document begins; a window's first token has position 0; the first document is exactly 1536 tokens long and no document is longer.
All inputs are finite; a program needn't handle non-finite values.
Results may differ from a plain program's by a relative error of at most 0.013.
The roundings to bfloat16 on the way count: a program that leaves them out, or rounds other values in their place, can miss the bound.
Values may be sent and summed in bfloat16 or wider, within the bound.
A program may use at most 128 MiB of HBM per device.

v0:
```python
import jax
import jax.numpy as jnp
from jax import lax
from jax.sharding import PartitionSpec as P

QL = 1536
KVL = 512
ROPE = 64
NOPE = 128
VD = 128


def rope_tables(positions):
    half_rope = ROPE // 2
    rotation_rates = 10000.0 ** (-jnp.arange(half_rope, dtype=jnp.float32) / half_rope)
    angles = positions.astype(jnp.float32)[:, None] * rotation_rates[None, :]
    return (jnp.cos(angles), jnp.sin(angles))


def rotate(vector, cosine, sine_table):
    half_rope = ROPE // 2
    front_half = vector[..., :half_rope]
    back_half = vector[..., half_rope:]
    return jnp.concatenate(
        [
            front_half * cosine - back_half * sine_table,
            front_half * sine_table + back_half * cosine,
        ],
        -1,
    )


def unrotate(vector, cosine, sine_table):
    half_rope = ROPE // 2
    front_half = vector[..., :half_rope]
    back_half = vector[..., half_rope:]
    return jnp.concatenate(
        [
            front_half * cosine + back_half * sine_table,
            back_half * cosine - front_half * sine_table,
        ],
        -1,
    )


def shards(query_latent, kv_latent, query_up, kv_up, out_grad, positions):
    tok_dev = query_latent.shape[1]
    heads_dev = query_up.shape[1] // (NOPE + ROPE)
    tokens = tok_dev * lax.axis_size("seq")
    first_row = lax.axis_index("seq") * tok_dev
    local_latent = query_latent[0]
    all_positions = positions[0]
    local_positions = lax.dynamic_slice_in_dim(all_positions, first_row, tok_dev)
    token_index = jnp.arange(tokens, dtype=jnp.int32)
    query_index = first_row + jnp.arange(tok_dev, dtype=jnp.int32)
    visible = (token_index[None, :] <= query_index[:, None]) & (
        local_positions[:, None] - all_positions[None, :]
        == query_index[:, None] - token_index[None, :]
    )
    cosine, sine_table = rope_tables(local_positions)
    softmax_scale = (NOPE + ROPE) ** (-0.5)
    query_weight = query_up.reshape(QL, heads_dev, NOPE + ROPE)
    kv_weight = kv_up.reshape(KVL, heads_dev, NOPE + VD)
    grad_heads = out_grad[0].reshape(tok_dev, heads_dev, VD).transpose(1, 0, 2)
    shard_rows = lax.all_gather(kv_latent[0], "seq", axis=0, tiled=True)
    projected = jnp.einsum(
        "tc,chd->htd", shard_rows[:, :KVL], kv_weight, preferred_element_type=jnp.float32
    )
    key_rope = jnp.broadcast_to(
        shard_rows[None, :, KVL:].astype(jnp.float32), (heads_dev, shard_rows.shape[0], ROPE)
    )
    key_value = jnp.concatenate(
        [projected[..., :NOPE], key_rope, projected[..., NOPE:]], -1
    ).astype(jnp.bfloat16)
    key_rows = key_value[..., : NOPE + ROPE]
    values = key_value[..., NOPE + ROPE :]
    projected_q = jnp.einsum(
        "tq,qhd->htd", local_latent, query_weight, preferred_element_type=jnp.float32
    )
    queries = jnp.concatenate(
        [projected_q[..., :NOPE], rotate(projected_q[..., NOPE:], cosine, sine_table)], -1
    ).astype(jnp.bfloat16)
    scores = (
        jnp.einsum("hqd,hkd->hqk", queries, key_rows, preferred_element_type=jnp.float32)
        * softmax_scale
    )
    scores = jnp.where(visible[None], scores, -jnp.inf)
    row_max = jnp.max(scores, 2, keepdims=True)
    exponent = jnp.exp(scores - row_max)
    attention = exponent / jnp.sum(exponent, 2, keepdims=True)
    prob_grad = jnp.einsum("hqd,hkd->hqk", grad_heads, values, preferred_element_type=jnp.float32)
    row_inner = jnp.sum(attention * prob_grad, 2, keepdims=True)
    score_grad = (attention * (prob_grad - row_inner) * softmax_scale).astype(jnp.bfloat16)
    attention_low = attention.astype(jnp.bfloat16)
    value_grad = jnp.einsum(
        "hqk,hqd->hkd", attention_low, grad_heads, preferred_element_type=jnp.float32
    ).astype(jnp.bfloat16)
    query_rows_grad = jnp.einsum(
        "hqk,hkd->hqd", score_grad, key_rows, preferred_element_type=jnp.float32
    )
    key_grad = jnp.einsum(
        "hqk,hqd->hkd", score_grad, queries, preferred_element_type=jnp.float32
    ).astype(jnp.bfloat16)
    head_query_grad = jnp.concatenate(
        [query_rows_grad[..., :NOPE], unrotate(query_rows_grad[..., NOPE:], cosine, sine_table)], -1
    ).astype(jnp.bfloat16)
    query_term = jnp.einsum(
        "htd,qhd->tq", head_query_grad, query_weight, preferred_element_type=jnp.float32
    )
    query_grad = lax.psum(query_term, "head").astype(jnp.bfloat16)[None]
    weight_term = jnp.einsum(
        "tq,htd->qhd", local_latent, head_query_grad, preferred_element_type=jnp.float32
    )
    weight_term = weight_term.reshape(QL, heads_dev * (NOPE + ROPE))
    kv_rows_grad = jnp.concatenate([key_grad[..., :NOPE], value_grad], -1)
    rope_grad = key_grad[..., NOPE:]
    latent_part = jnp.einsum(
        "htd,chd->tc", kv_rows_grad, kv_weight, preferred_element_type=jnp.float32
    )
    latent_grad = lax.psum_scatter(
        jnp.concatenate([latent_part, jnp.sum(rope_grad.astype(jnp.float32), 0)], -1),
        ("seq", "head"),
        scatter_dimension=0,
        tiled=True,
    )
    weight_grad = lax.psum_scatter(weight_term, ("rep", "seq"), scatter_dimension=0, tiled=True)
    return (query_grad, latent_grad.astype(jnp.bfloat16)[None], weight_grad.astype(jnp.bfloat16))


def solution(mesh):
    return jax.shard_map(
        shards,
        mesh=mesh,
        in_specs=(
            P("rep", "seq", None),
            P("rep", "seq", None),
            P(None, "head"),
            P(None, "head"),
            P("rep", "seq", "head"),
            P("rep", None),
        ),
        out_specs=(
            P("rep", "seq", None),
            P("rep", ("seq", "head"), None),
            P(("rep", "seq"), "head"),
        ),
        check_vma=False,
    )
```

profile of v0, /device:TPU:128, one launch (start us, length us, event | category | flops | bytes accessed | tf_op | source)
XLA Modules:
  0.0 1036.1 jit_solution(3629060452253005470)
XLA Ops:
  7.2 0.0 copy-start
  7.2 0.0 all-gather.3.cloned.1.call-start
  7.2 1.7 copy.33
  9.0 0.0 all-gather.3.cloned.1.call-update
  9.0 0.0 reduce-scatter.7.cloned.1.call-start
  9.0 1.1 copy.48
  10.2 0.0 copy-start.3
  10.2 6.7 copy.32
  16.9 0.0 copy-done
  16.9 3.7 convolution_bitcast_fusion.1
  20.7 0.0 copy-done.3
  20.7 0.1 multiply_cosine_fusion
  20.9 1.2 fusion.30
  22.1 76.3 %all-gather.3.cloned.1.call-done = bf16[1,2048,576]{2,1,0:T(8,128)(2,1)} async-done(((bf16[1,128,576]{2,1,0:T(8,128)(2,1)}), bf16[1,2048,576]{2,1,0:T(8,128)(2,1)}) %all-gather.3.cloned.1.call-update) | async-done | bytes 2359312 | tf_op jit(solution)/shard_map/all_gather | solution.py:65
  98.4 1.1 slice.66
  99.4 0.2 copy.35
  99.6 6.8 convert_bitcast_fusion
  106.5 0.5 slice.65
  107.0 0.0 copy-start.1
  107.0 4.5 fusion.12
  111.5 0.2 broadcast_in_dim.15
  111.8 0.0 copy-done.1
  111.8 0.0 copy-start.2
  111.8 2.0 fusion.11
  113.8 0.0 copy-done.2
  113.8 5.7 fusion.47
  119.4 6.7 fusion.19
  126.1 15.9 %convolution_convert_fusion = bf16[8,2048,192]{1,2,0:T(8,128)(2,1)} fusion(f32[8,2048,128]{1,2,0:T(8,128)} %fusion.12, bf16[8,128,32]{1,2,0:T(8,128)(2,1)S(1)} %get-tuple-element.17, bf16[8,128,32]{1,2,0:T(8,128)(2,1)S(1)} %get-tuple-element.16, bf16[8,128,128]{1,2,0:T(8,128)(2,1)S(1)} %slice.89, f32[8,128,2048]{2,1,0:T(8,128)} %get-tuple-element.21, ...), kind=kOutput, calls=%fused_computation.19 | convolution fusion | flops 824314880 | bytes 23465984 | tf_op jit(solution)/shard_map/hqk,hqd->hkd/dot_general | solution.py:101
  142.0 0.0 slice-start
  142.0 0.0 copy-start.4
  142.0 0.0 copy-start.5
  142.0 2.1 convert_reduce_fusion
  144.2 0.7 slice-done
  144.8 0.7 copy-done.4
  145.5 1.2 copy-done.5
  146.7 4.5 fusion.23
  151.2 2.7 pad_maximum_fusion.3
  153.9 5.8 copy.49
  159.7 0.0 reduce-scatter.7.cloned.1.call-update
  159.7 0.0 reduce-scatter.5.cloned.1.call-start
  159.8 14.5 %fusion.10 = f32[8,128,192]{1,2,0:T(8,128)S(1)} fusion(bf16[8,2048,64]{1,2,0:T(8,128)(2,1)S(1)} %broadcast_in_dim.15, bf16[8,2048,128]{1,2,0:T(8,128)(2,1)} %copy-done.1, f32[8,2048,128]{1,2,0:T(8,128)} %fusion.12, f32[8,128,2048]{2,1,0:T(8,128)} %get-tuple-element.21, f32[8,128]{1,0:T(8,128)S(1)} %get-tuple-element.20), kind=kOutput, calls=%fused_computation.16 | convolution fusion | flops 832572416 | bytes 23859200 | tf_op jit(solution)/shard_map/hqk,hkd->hqd/dot_general | solution.py:98
  174.4 5.0 fusion.31
  179.4 9.6 copy.42
  189.0 0.0 reduce-scatter.5.cloned.1.call-update
  189.1 3.2 convolution_bitcast_fusion
  192.2 41.6 %all-reduce.1 = bf16[128,1536]{1,0:T(8,128)(2,1)} all-reduce(f32[128,1536]{1,0:T(8,128)S(1)} %convolution_bitcast_fusion), channel_id=1, replica_groups=mesh['rep'=2,'seq'=16,'head'=8] {'head'}, use_global_device_ids=true, to_apply=%region_3.4 | all-reduce | flops 196608 | bytes 1179648 | tf_op jit(solution)/shard_map/psum | solution.py:110
  233.8 635.0 %reduce-scatter.7.cloned.1.call-done = f32[16,576]{1,0:T(8,128)} async-done(((f32[2048,576]{1,0:T(8,128)}), f32[16,576]{1,0:T(8,128)}) %reduce-scatter.7.cloned.1.call-update) | async-done | bytes 36880
  868.8 0.9 copy.50
  869.7 0.7 copy.43
  870.5 157.4 %reduce-scatter.5.cloned.1.call-done = f32[48,1536]{1,0:T(8,128)} async-done(((f32[1536,1536]{1,0:T(8,128)}), f32[48,1536]{1,0:T(8,128)}) %reduce-scatter.5.cloned.1.call-update) | async-done | bytes 294928 | tf_op jit(solution)/shard_map/reduce_scatter | solution.py:126
  1027.9 1.6 convert_element_type.44
  (7 shorter events, 0.2 us)
Async XLA Ops:
  7.2 9.7 copy-start
  7.2 91.2 %all-gather.3.cloned.1.call-start = ((), (), s32[]{:S(2)}) async-start(), calls=%async_computation.3 | async-start | bytes 2785280 | tf_op jit(solution)/shard_map/all_gather | solution.py:65
  9.0 859.8 %reduce-scatter.7.cloned.1.call-start = ((), (), s32[]{:S(2)}) async-start(), calls=%async_computation.4 | async-start | bytes 5283840
  10.2 10.5 %copy-start.3 = (s32[1,2048]{1,0:T(1,128)S(1)}, s32[1,2048]{1,0:T(1,128)}, u32[]{:S(2)}) copy-start(s32[1,2048]{1,0:T(1,128)} %param.11) | copy-start | bytes 24580
  107.0 4.8 copy-start.1
  111.8 2.0 copy-start.2
  142.0 2.8 slice-start
  142.0 3.5 copy-start.4
  142.0 4.7 copy-start.5
  159.7 868.2 %reduce-scatter.5.cloned.1.call-start = ((), (), s32[]{:S(2)}) async-start(), calls=%async_computation.2 | async-start | bytes 9732096 | tf_op jit(solution)/shard_map/reduce_scatter | solution.py:126
Sparse Core Ops, SparseCore 0:
  10.6 87.7 all-gather.2
  159.8 708.9 reduce-scatter.6
  873.3 154.5 reduce-scatter.4
where the time goes:
time: 1040 us
  waiting for transfers between devices  869 us (84%)
  matrix products  66.8 us (6%)
  blocking collectives  41.6 us (4%)
  local copies, waits for them, and re-layouts  31.3 us (3%)
  between operations  14 us (1%)
  other arithmetic  13.5 us (1%)
    unnamed x4, waiting for transfers between devices  635 us
    reduce_scatter x1, waiting for transfers between devices, shards(): lax.psum_scatter(weight_term, ('rep', 'seq'), scatter_dimension=0, tiled=...  157 us
    all_gather x1, waiting for transfers between devices, shards(): shard_rows = lax.all_gather(kv_latent[0], 'seq', axis=0, tiled=True)  76.3 us
    psum x1, blocking collectives, shards(): query_grad = lax.psum(query_term, 'head').astype(jnp.bfloat16)[None]  41.6 us
  transfers between devices with their start and end apart: 3, of which 3 were waited for; matrix products, arithmetic and copies ran while one was open for 5% of the time, Pallas kernels for 0%

commit v1 on v0

v1 whole, which is shorter than its diff:
```python
import jax
import jax.numpy as jnp
from jax import lax
from jax.experimental import pallas as pl
from jax.experimental.pallas import tpu as pltpu
from jax.sharding import PartitionSpec as P

QL = 1536
KVL = 512
ROPE = 64
NOPE = 128
VD = 128
HEADS = 8
TOK = 128
SLOTS = 12
SUB = 16
LAT = 640
KEYS = SLOTS * TOK
FIRST = 12
BF = jnp.bfloat16
F32 = jnp.float32
MESH = pl.DeviceIdType.MESH
VMEM_LIMIT = 63 * 1024 * 1024


def place():
    return lax.axis_index("rep"), lax.axis_index("seq"), lax.axis_index("head")


def group_base(s):
    return jnp.where(s < FIRST, 0, FIRST)


def z_partner(s):
    return s + 2 - 4 * lax.rem(lax.div(s, 2), 2)


def peer_rows(s):
    return lax.rem(lax.div(s, 2), 2)


def covered(z, zb, j):
    return lax.rem(jnp.where(zb == 0, z - j + 8, z + j), 8)


def remote(src, dst, send, recv, device):
    return pltpu.make_async_remote_copy(
        src_ref=src, dst_ref=dst, send_sem=send, recv_sem=recv, device_id=device, device_id_type=MESH
    )


def greet(devices_list):
    barrier = pltpu.get_barrier_semaphore()
    for device in devices_list:
        pl.semaphore_signal(barrier, inc=1, device_id=device, device_id_type=MESH)
    return barrier


def gather_kernel(kv_ref, xt_ref, lat_ref, xg_ref, s1, r1, s2, r2, sx, rx, lsem):
    r, s, h = place()
    base = group_base(s)
    slot = s - base
    z, zb = lax.div(s, 2), peer_rows(s)
    big = s < FIRST
    other = z_partner(s)
    quad = [(1 - r, s, h), (r, other, h), (1 - r, other, h)]
    plane = [(r, s, lax.rem(h + d, HEADS)) for d in range(1, HEADS)]

    barrier = greet(plane + quad)

    @pl.when(big)
    def _():
        for d in range(1, SLOTS):
            pl.semaphore_signal(
                barrier, inc=1, device_id=(r, lax.rem(slot + d, SLOTS), h), device_id_type=MESH
            )
        pl.semaphore_wait(barrier, SLOTS - 1 + 10)

    @pl.when(jnp.logical_not(big))
    def _():
        for d in range(1, 4):
            pl.semaphore_signal(
                barrier, inc=1, device_id=(r, FIRST + lax.rem(slot + d, 4), h), device_id_type=MESH
            )
        pl.semaphore_wait(barrier, 3 + 10)

    def to_seq(d, n):
        return remote(
            kv_ref.at[h], lat_ref.at[slot, h], s1.at[d], r1.at[d], (r, base + lax.rem(slot + d, n), h)
        )

    def from_seq(d, n):
        source = lax.rem(slot - d + n, n)
        return remote(kv_ref.at[h], lat_ref.at[source, h], s1.at[d], r1.at[d], (r, base + source, h))

    @pl.when(big)
    def _():
        for d in range(1, SLOTS):
            to_seq(d, SLOTS).start()

    @pl.when(jnp.logical_not(big))
    def _():
        for d in range(1, 4):
            to_seq(d, 4).start()
        for k in range(4, SLOTS):
            pltpu.make_async_copy(kv_ref.at[h], lat_ref.at[k, h], lsem.at[k]).start()

    pltpu.make_async_copy(kv_ref.at[h], lat_ref.at[slot, h], lsem.at[0]).start()

    mine = 2 * r + zb
    for k, (dr, dz) in enumerate(((1, 0), (0, 1), (1, 1))):
        pr = lax.rem(r + dr, 2)
        pzb = lax.rem(zb + dz, 2)
        ps = jnp.where(dz == 1, other, s)
        for j in range(4):
            zz = covered(lax.div(ps, 2), pzb, j)
            remote(
                xt_ref.at[pr, zz], xg_ref.at[mine, j], sx.at[k, j], rx.at[k, j], (pr, ps, h)
            ).start()
    for j in range(4):
        pltpu.make_async_copy(xt_ref.at[r, covered(z, zb, j)], xg_ref.at[mine, j], sx.at[3, j]).start()

    @pl.when(big)
    def _():
        for d in range(1, SLOTS):
            from_seq(d, SLOTS).wait_recv()

    @pl.when(jnp.logical_not(big))
    def _():
        for d in range(1, 4):
            from_seq(d, 4).wait_recv()
        for k in range(4, SLOTS):
            pltpu.make_async_copy(kv_ref.at[h], lat_ref.at[k, h], lsem.at[k]).wait()

    pltpu.make_async_copy(kv_ref.at[h], lat_ref.at[slot, h], lsem.at[0]).wait()

    for d in range(1, HEADS):
        remote(
            lat_ref.at[:, h], lat_ref.at[:, h], s2.at[d], r2.at[d], (r, s, lax.rem(h + d, HEADS))
        ).start()

    for k, (dr, dz) in enumerate(((1, 0), (0, 1), (1, 1))):
        source = 2 * lax.rem(r + dr, 2) + lax.rem(zb + dz, 2)
        for j in range(4):
            copy = remote(xt_ref.at[0, 0], xg_ref.at[source, j], sx.at[k, j], rx.at[k, j], (r, s, h))
            copy.wait_recv()
            copy.wait_send()
    for j in range(4):
        pltpu.make_async_copy(xt_ref.at[0, 0], xg_ref.at[mine, j], sx.at[3, j]).wait()
    for d in range(1, HEADS):
        source = lax.rem(h - d + HEADS, HEADS)
        copy = remote(lat_ref.at[:, h], lat_ref.at[:, source], s2.at[d], r2.at[d], (r, s, source))
        copy.wait_recv()
        copy.wait_send()

    @pl.when(big)
    def _():
        for d in range(1, SLOTS):
            to_seq(d, SLOTS).wait_send()

    @pl.when(jnp.logical_not(big))
    def _():
        for d in range(1, 4):
            to_seq(d, 4).wait_send()


def gather(kv, xt):
    dma = pltpu.SemaphoreType.DMA
    anyspace = pl.BlockSpec(memory_space=pl.ANY)
    return pl.pallas_call(
        gather_kernel,
        out_shape=(
            jax.ShapeDtypeStruct((SLOTS, HEADS, SUB, LAT), BF),
            jax.ShapeDtypeStruct((4, 4, 96, TOK), BF),
        ),
        in_specs=[anyspace] * 2,
        out_specs=(anyspace, anyspace),
        scratch_shapes=[
            dma((SLOTS,)), dma((SLOTS,)), dma((HEADS,)), dma((HEADS,)), dma((4, 4)), dma((4, 4)), dma((SLOTS,)),
        ],
        compiler_params=pltpu.CompilerParams(collective_id=0, has_side_effects=True),
        name="gather_latents",
    )(kv, xt)


NT = (((1,), (1,)), ((), ()))
TN = (((0,), (0,)), ((), ()))
NN = (((1,), (0,)), ((), ()))
PAIRS = HEADS // 2
ROWS = 128


def dot(a, b, dims):
    return lax.dot_general(a, b, dims, preferred_element_type=F32)


def swap_halves(v):
    lane = lax.broadcasted_iota(jnp.int32, v.shape, 1)
    half = ROPE // 2
    return jnp.where(lax.rem(lane, ROPE) < half, pltpu.roll(v, TOK - half, 1), pltpu.roll(v, half, 1))


def attention_kernel(
    x_ref, wq_ref, wkv_ref, do_ref, lat_ref, cos_ref, sin_ref, bounds_ref,
    dq_ref, dl_ref, qt_ref,
    a_s, r_s, kv_s, sp_s, sr_s, dp_s, dkv_s, rope_s,
):
    scale = (NOPE + ROPE) ** (-0.5)
    cosine, sine = cos_ref[...], sin_ref[...]
    left = lax.broadcasted_iota(jnp.int32, (TOK, TOK), 1) < ROPE
    projected = dot(x_ref[...], wq_ref[...], NN)
    for g in range(PAIRS):
        one, mid, last = (projected[:, 384 * g + TOK * k : 384 * g + TOK * (k + 1)] for k in range(3))
        two = jnp.where(left, pltpu.roll(mid, ROPE, 1), pltpu.roll(last, ROPE, 1))
        none = jnp.zeros((TOK, TOK), BF)
        for k, nope in enumerate((one, two)):
            i = 2 * g + k
            a_s[i, :TOK, :TOK] = nope.astype(BF)
            a_s[i, :TOK, TOK:] = none
            a_s[i, TOK:, :TOK] = none
            a_s[i, TOK:, TOK:] = do_ref[:, TOK * i : TOK * (i + 1)]
        r_s[g, :TOK, :] = jnp.where(left, mid * cosine + swap_halves(mid) * sine, 0.0).astype(BF)
        r_s[g, TOK:, :] = jnp.where(left, 0.0, last * cosine + swap_halves(last) * sine).astype(BF)
    rope_s[...] = jnp.zeros_like(rope_s)

    low = bounds_ref[0:1, :]
    high = bounds_ref[1:2, :]
    steps = KEYS // ROWS
    fold = (ROWS // 8, 8, TOK)
    both = range(2)

    def pair(g, carry):
        columns = pl.ds(pl.multiple_of(512 * g, 512), 512)
        kv_s[...] = dot(lat_ref[:, :KVL], wkv_ref[:, columns], NN).astype(BF)
        for k in both:
            sp_s[k] = dot(kv_s[:, 256 * k : 256 * (k + 1)], a_s[2 * g + k], NT)
        sr_s[...] = dot(lat_ref[:, KVL:], r_s[g], NT)

        def first(c, tops):
            at = pl.ds(pl.multiple_of(c * ROWS, ROWS), ROWS)
            key = c * ROWS + lax.broadcasted_iota(jnp.int32, (ROWS, TOK), 0)
            seen = (key >= low) & (key <= high)
            out = []
            for k in both:
                value = (sp_s[k, at, :TOK] + sr_s[at, TOK * k : TOK * (k + 1)]) * scale
                value = jnp.where(seen, value, -jnp.inf)
                sp_s[k, at, :TOK] = value
                out.append(jnp.maximum(tops[k], jnp.max(value.reshape(fold), 0)))
            return tuple(out)

        start = jnp.full((8, TOK), -jnp.inf, F32)
        tops = lax.fori_loop(0, steps, first, (start, start))
        tops = [jnp.max(top, 0, keepdims=True) for top in tops]

        def second(c, sums):
            at = pl.ds(pl.multiple_of(c * ROWS, ROWS), ROWS)
            out = []
            for k in both:
                value = jnp.exp(sp_s[k, at, :TOK] - tops[k])
                sp_s[k, at, :TOK] = value
                out.append(sums[2 * k] + jnp.sum(value.reshape(fold), 0))
                out.append(sums[2 * k + 1] + jnp.sum((value * sp_s[k, at, TOK:]).reshape(fold), 0))
            return tuple(out)

        zero = jnp.zeros((8, TOK), F32)
        sums = lax.fori_loop(0, steps, second, (zero,) * 4)
        inverse = [1.0 / jnp.sum(sums[2 * k], 0, keepdims=True) for k in both]
        inner = [jnp.sum(sums[2 * k + 1], 0, keepdims=True) * inverse[k] for k in both]

        def third(c, nothing):
            at = pl.ds(pl.multiple_of(c * ROWS, ROWS), ROWS)
            for k in both:
                weight = sp_s[k, at, :TOK] * inverse[k]
                dp_s[k, at, TOK:] = weight.astype(BF)
                dp_s[k, at, :TOK] = (weight * (sp_s[k, at, TOK:] - inner[k]) * scale).astype(BF)
            return nothing

        lax.fori_loop(0, steps, third, 0)
        nopes, ropes = [], []
        for k in both:
            score_grad = dp_s[k, :, :TOK]
            nopes.append(dot(score_grad, kv_s[:, 256 * k : 256 * k + NOPE], TN))
            chunk = dot(score_grad, lat_ref[:, KVL:], TN)
            ropes.append(chunk * cosine - swap_halves(chunk) * sine)
            dkv_s[g, :, 256 * k : 256 * (k + 1)] = dot(dp_s[k], a_s[2 * g + k], NN).astype(BF)
        second_nope = pltpu.roll(nopes[1], ROPE, 1)
        joined = jnp.concatenate(
            [nopes[0], jnp.where(left, ropes[0], second_nope), jnp.where(left, second_nope, ropes[1])], 1
        )
        dq_ref[:, pl.ds(pl.multiple_of(384 * g, 384), 384)] = joined.astype(BF)
        grads = jnp.concatenate([dp_s[0, :, :TOK], dp_s[1, :, :TOK]], 1)
        rope_s[...] += dot(grads, r_s[g], NN).astype(BF).astype(F32)
        return carry

    lax.fori_loop(0, PAIRS, pair, 0)
    qt_ref[...] = dot(dq_ref[...], wq_ref[...], NT).astype(BF)

    def latents(c, nothing):
        at = pl.ds(pl.multiple_of(c * 512, 512), 512)
        joined = jnp.concatenate([dkv_s[g, at, :] for g in range(PAIRS)], 1)
        dl_ref[at, :KVL] = dot(joined, wkv_ref[...], NT).astype(BF)
        rope = rope_s[at, :]
        dl_ref[at, KVL:] = (rope + pltpu.roll(rope, ROPE, 1)).astype(BF)
        return nothing

    lax.fori_loop(0, KEYS // 512, latents, 0)


def attention(x, wq, wkv, do, lat, cosine, sine, bounds):
    return pl.pallas_call(
        attention_kernel,
        out_shape=(
            jax.ShapeDtypeStruct((TOK, QL), BF),
            jax.ShapeDtypeStruct((KEYS, LAT), BF),
            jax.ShapeDtypeStruct((TOK, QL), BF),
        ),
        in_specs=[pl.BlockSpec(memory_space=pltpu.VMEM)] * 8,
        out_specs=(pl.BlockSpec(memory_space=pltpu.VMEM),) * 3,
        scratch_shapes=[
            pltpu.VMEM((HEADS, 2 * TOK, 2 * TOK), BF),
            pltpu.VMEM((PAIRS, 2 * TOK, TOK), BF),
            pltpu.VMEM((KEYS, 512), BF),
            pltpu.VMEM((2, KEYS, 2 * TOK), F32),
            pltpu.VMEM((KEYS, 2 * TOK), F32),
            pltpu.VMEM((2, KEYS, 2 * TOK), BF),
            pltpu.VMEM((PAIRS, KEYS, 512), BF),
            pltpu.VMEM((KEYS, TOK), F32),
        ],
        compiler_params=pltpu.CompilerParams(vmem_limit_bytes=VMEM_LIMIT),
        name="attention_backward",
    )(x, wq, wkv, do, lat, cosine, sine, bounds)


def exchange_kernel(dq_ref, dl_ref, qt_ref, dg_ref, rl_ref, rq_ref, ss, rs, sq, rq, sd, rd, lsem):
    r, s, h = place()
    zb = peer_rows(s)
    other = z_partner(s)
    quad = [(1 - r, s, h), (r, other, h), (1 - r, other, h)]
    plane = [(r, s, lax.rem(h + d, HEADS)) for d in range(1, HEADS)]
    barrier = greet(plane + quad)
    pl.semaphore_wait(barrier, 10)
    mine = 2 * r + zb
    for k, device in enumerate(quad):
        remote(dq_ref, dg_ref.at[mine], sd.at[k], rd.at[k], device).start()
    for d in range(1, HEADS):
        peer = lax.rem(h + d, HEADS)
        remote(dl_ref.at[:, peer], rl_ref.at[h], ss.at[d], rs.at[d], (r, s, peer)).start()
        remote(qt_ref.at[peer], rq_ref.at[h], sq.at[d], rq.at[d], (r, s, peer)).start()
    local = [
        pltpu.make_async_copy(dq_ref, dg_ref.at[mine], lsem.at[0]),
        pltpu.make_async_copy(dl_ref.at[:, h], rl_ref.at[h], lsem.at[1]),
        pltpu.make_async_copy(qt_ref.at[h], rq_ref.at[h], lsem.at[2]),
    ]
    for copy in local:
        copy.start()
    for copy in local:
        copy.wait()
    for k, (dr, dz) in enumerate(((1, 0), (0, 1), (1, 1))):
        source = 2 * lax.rem(r + dr, 2) + lax.rem(zb + dz, 2)
        copy = remote(dq_ref, dg_ref.at[source], sd.at[k], rd.at[k], quad[k])
        copy.wait_recv()
        copy.wait_send()
    for d in range(1, HEADS):
        source = lax.rem(h - d + HEADS, HEADS)
        copy = remote(dl_ref.at[:, h], rl_ref.at[source], ss.at[d], rs.at[d], (r, s, source))
        copy.wait_recv()
        copy.wait_send()
        copy = remote(qt_ref.at[h], rq_ref.at[source], sq.at[d], rq.at[d], (r, s, source))
        copy.wait_recv()
        copy.wait_send()


def exchange(dq, dl, qt):
    dma = pltpu.SemaphoreType.DMA
    anyspace = pl.BlockSpec(memory_space=pl.ANY)
    return pl.pallas_call(
        exchange_kernel,
        out_shape=(
            jax.ShapeDtypeStruct((4, TOK, QL), BF),
            jax.ShapeDtypeStruct((HEADS, SLOTS, SUB, LAT), BF),
            jax.ShapeDtypeStruct((HEADS, SUB, QL), BF),
        ),
        in_specs=[anyspace] * 3,
        out_specs=(anyspace,) * 3,
        scratch_shapes=[dma((HEADS,)), dma((HEADS,)), dma((HEADS,)), dma((HEADS,)), dma((3,)), dma((3,)), dma((3,))],
        compiler_params=pltpu.CompilerParams(collective_id=1, has_side_effects=True),
        name="exchange_terms",
    )(dq, dl, qt)


def combine_kernel(xg_ref, dg_ref, rl_ref, rq_ref, w_ref, ls_ref, qs_ref):
    left = jnp.concatenate([xg_ref[k].reshape(4 * 96, TOK) for k in range(4)], 1)
    right = dg_ref[...].reshape(4 * TOK, QL)
    w_ref[...] = dot(left, right, NN).astype(BF)
    total = rq_ref[0].astype(F32)
    for k in range(1, HEADS):
        total += rq_ref[k].astype(F32)
    qs_ref[...] = total.astype(BF)
    for c in range(SLOTS):
        total = rl_ref[0, c].astype(F32)
        for k in range(1, HEADS):
            total += rl_ref[k, c].astype(F32)
        ls_ref[c] = total.astype(BF)


def combine(xg, dg, rl, rq):
    return pl.pallas_call(
        combine_kernel,
        out_shape=(
            jax.ShapeDtypeStruct((4 * 96, QL), BF),
            jax.ShapeDtypeStruct((SLOTS, SUB, LAT), BF),
            jax.ShapeDtypeStruct((SUB, QL), BF),
        ),
        in_specs=[pl.BlockSpec(memory_space=pltpu.VMEM)] * 4,
        out_specs=(pl.BlockSpec(memory_space=pltpu.VMEM),) * 3,
        compiler_params=pltpu.CompilerParams(vmem_limit_bytes=VMEM_LIMIT),
        name="combine_terms",
    )(xg, dg, rl, rq)


def source_z(z, j):
    down = lax.rem(z + j, 8)
    up = lax.rem(z - j + 8, 8)
    return jnp.where(lax.rem(down, 2) == 0, down, up)


def deliver_kernel(w_ref, ls_ref, qs_ref, rw_ref, rl_ref, qg_ref, sw, rw, sl, rl, sq, rq, lsem):
    r, s, h = place()
    base = group_base(s)
    slot = s - base
    big = s < FIRST
    z, zb, yh = lax.div(s, 2), peer_rows(s), lax.rem(s, 2)
    plane = [(r, s, lax.rem(h + d, HEADS)) for d in range(1, HEADS)]
    steps = [(j, y) for j in range(4) for y in range(2)][1:]
    owners = [(j, y, (r, 2 * covered(z, zb, j) + lax.rem(yh + y, 2), h)) for j, y in steps]
    sources = [(j, y, (r, 2 * source_z(z, j) + lax.rem(yh + y, 2), h)) for j, y in steps]
    barrier = greet(plane + [device for _, _, device in sources])

    @pl.when(big)
    def _():
        for d in range(1, SLOTS):
            pl.semaphore_signal(
                barrier, inc=1, device_id=(r, lax.rem(slot + d, SLOTS), h), device_id_type=MESH
            )
        pl.semaphore_wait(barrier, SLOTS - 1 + 14)

    @pl.when(jnp.logical_not(big))
    def _():
        for d in range(1, 4):
            pl.semaphore_signal(
                barrier, inc=1, device_id=(r, FIRST + lax.rem(slot + d, 4), h), device_id_type=MESH
            )
        pl.semaphore_wait(barrier, 3 + 14)

    for j, y, device in owners:
        remote(w_ref.at[j, lax.rem(yh + y, 2)], rw_ref.at[j, y], sw.at[j, y], rw.at[j, y], device).start()

    def send_latent(d, n):
        peer = lax.rem(slot + d, n)
        return remote(ls_ref.at[peer], rl_ref.at[slot], sl.at[d], rl.at[d], (r, base + peer, h))

    def take_latent(d, n):
        peer = lax.rem(slot - d + n, n)
        return remote(ls_ref.at[0], rl_ref.at[peer], sl.at[d], rl.at[d], (r, base + peer, h))

    @pl.when(big)
    def _():
        for d in range(1, SLOTS):
            send_latent(d, SLOTS).start()

    @pl.when(jnp.logical_not(big))
    def _():
        for d in range(1, 4):
            send_latent(d, 4).start()

    for d in range(1, HEADS):
        remote(qs_ref, qg_ref.at[h], sq.at[d], rq.at[d], (r, s, lax.rem(h + d, HEADS))).start()
    local = [
        pltpu.make_async_copy(w_ref.at[0, yh], rw_ref.at[0, 0], lsem.at[0]),
        pltpu.make_async_copy(ls_ref.at[slot], rl_ref.at[slot], lsem.at[1]),
        pltpu.make_async_copy(qs_ref, qg_ref.at[h], lsem.at[2]),
    ]
    for copy in local:
        copy.start()
    for copy in local:
        copy.wait()

    for d in range(1, HEADS):
        source = lax.rem(h - d + HEADS, HEADS)
        copy = remote(qs_ref, qg_ref.at[source], sq.at[d], rq.at[d], (r, s, source))
        copy.wait_recv()
        copy.wait_send()

    @pl.when(big)
    def _():
        for d in range(1, SLOTS):
            take_latent(d, SLOTS).wait_recv()
            send_latent(d, SLOTS).wait_send()

    @pl.when(jnp.logical_not(big))
    def _():
        for d in range(1, 4):
            take_latent(d, 4).wait_recv()
            send_latent(d, 4).wait_send()

    for j, y, device in sources:
        copy = remote(w_ref.at[j, 0], rw_ref.at[j, y], sw.at[j, y], rw.at[j, y], device)
        copy.wait_recv()
        copy.wait_send()


def deliver(w, ls, qs):
    dma = pltpu.SemaphoreType.DMA
    anyspace = pl.BlockSpec(memory_space=pl.ANY)
    return pl.pallas_call(
        deliver_kernel,
        out_shape=(
            jax.ShapeDtypeStruct((4, 2, 48, QL), BF),
            jax.ShapeDtypeStruct((SLOTS, SUB, LAT), BF),
            jax.ShapeDtypeStruct((HEADS, SUB, QL), BF),
        ),
        in_specs=[anyspace] * 3,
        out_specs=(anyspace,) * 3,
        scratch_shapes=[
            dma((4, 2)), dma((4, 2)), dma((SLOTS,)), dma((SLOTS,)), dma((HEADS,)), dma((HEADS,)), dma((3,)),
        ],
        compiler_params=pltpu.CompilerParams(collective_id=2, has_side_effects=True),
        name="deliver_sums",
    )(w, ls, qs)


def finish_kernel(rw_ref, rl_ref, count_ref, w_ref, l_ref):
    total = rw_ref[0, 0].astype(F32)
    for k in range(1, 8):
        total += rw_ref[k // 2, k % 2].astype(F32)
    w_ref[...] = total.astype(BF)
    count = count_ref[0]
    total = jnp.zeros((SUB, LAT), F32)
    for k in range(SLOTS):
        total += jnp.where(k < count, rl_ref[k].astype(F32), 0.0)
    l_ref[...] = total[:, : KVL + ROPE].astype(BF)


def finish(rw, rl, count):
    return pl.pallas_call(
        finish_kernel,
        out_shape=(
            jax.ShapeDtypeStruct((48, QL), BF),
            jax.ShapeDtypeStruct((SUB, KVL + ROPE), BF),
        ),
        in_specs=[pl.BlockSpec(memory_space=pltpu.VMEM)] * 2 + [pl.BlockSpec(memory_space=pltpu.SMEM)],
        out_specs=(pl.BlockSpec(memory_space=pltpu.VMEM),) * 2,
        name="finish_sums",
    )(rw, rl, count)


def shards(query_latent, kv_latent, query_up, kv_up, out_grad, positions):
    s = lax.axis_index("seq")
    x = query_latent[0]
    first_row = s * TOK
    local_positions = lax.dynamic_slice_in_dim(positions[0], first_row, TOK)
    index = first_row + jnp.arange(TOK, dtype=jnp.int32) - group_base(s) * TOK
    bounds = jnp.stack([index - local_positions, index] + [index] * 6)
    half = ROPE // 2
    rates = 10000.0 ** (-jnp.arange(half, dtype=F32) / half)
    angles = local_positions.astype(F32)[:, None] * rates[None, :]
    cosine, sine = jnp.cos(angles), jnp.sin(angles)
    cosine_table = jnp.concatenate([cosine] * 4, 1)
    sine_table = jnp.concatenate([-sine, sine] * 2, 1)
    kv = jnp.concatenate([kv_latent[0], kv_latent[0][:, KVL:]], 1).reshape(HEADS, SUB, LAT)
    xt = x.T.reshape(2, 8, 96, TOK)

    lat, xg = gather(kv, xt)
    dq, dl, qt = attention(
        x, query_up, kv_up, out_grad[0], lat.reshape(KEYS, LAT), cosine_table, sine_table, bounds
    )
    dg, rl, rq = exchange(dq, dl.reshape(SLOTS, HEADS, SUB, LAT), qt.reshape(HEADS, SUB, QL))
    w, ls, qs = combine(xg, dg, rl, rq)
    rw, rlat, qg = deliver(w.reshape(4, 2, 48, QL), ls, qs)
    count = jnp.where(s < FIRST, SLOTS, 4).astype(jnp.int32).reshape(1)
    weight_grad, latent_grad = finish(rw, rlat, count)
    return qg.reshape(1, TOK, QL), latent_grad[None], weight_grad


def solution(mesh):
    return jax.shard_map(
        shards,
        mesh=mesh,
        in_specs=(
            P("rep", "seq", None),
            P("rep", "seq", None),
            P(None, "head"),
            P(None, "head"),
            P("rep", "seq", "head"),
            P("rep", None),
        ),
        out_specs=(
            P("rep", "seq", None),
            P("rep", ("seq", "head"), None),
            P(("rep", "seq"), "head"),
        ),
        check_vma=False,
    )
```

time: 1040 us -> 169 us (0.16)
  waiting for transfers between devices: 869 us -> 0 us
  Pallas kernels: 0 us -> 156 us
  matrix products: 66.8 us -> 0 us
  blocking collectives: 41.6 us -> 0 us
  local copies, waits for them, and re-layouts: 31.3 us -> 6.2 us
  between operations: 14 us -> 0.68 us
  other arithmetic: 13.5 us -> 2.55 us
    unnamed x4 -> x0, waiting for transfers between devices: 635 us -> none
    reduce_scatter x1 -> x0, waiting for transfers between devices: 157 us -> none  [shards(): lax.psum_scatter(weight_term, ('rep', 'seq'), scatter_dimension=0, tiled=...]
    pallas_call x0 -> x6, Pallas kernels: none -> 156 us  [the longest x1 47.8 us: deliver(): pl.pallas_call(deliver_kernel, out_shape=(jax.ShapeDtypeStruct((4, 2, 48,...]
    all_gather x1 -> x0, waiting for transfers between devices: 76.3 us -> none  [shards(): shard_rows = lax.all_gather(kv_latent[0], 'seq', axis=0, tiled=True)]
    dot_general x10 -> x0, matrix products: 66.8 us -> none  [the longest x1 15.9 us: shards(): jnp.einsum('hqk,hqd->hkd', score_grad, queries, preferred_element_type=jn...]
    psum x1 -> x0, blocking collectives: 41.6 us -> none  [shards(): query_grad = lax.psum(query_term, 'head').astype(jnp.bfloat16)[None]]
    unnamed x17 -> x2, local copies, waits for them, and re-layouts: 17.8 us -> 2.84 us
  transfers between devices with their start and end apart: 3 -> 0, of which waited for: 3 -> 0; matrix products, arithmetic and copies ran while one was open for 5% -> 0% of each run, Pallas kernels for 0% -> 0%
where the time goes in v1:
time: 169 us; the launch traced here: 166 us
  Pallas kernels  156 us (92%)
  local copies, waits for them, and re-layouts  6.2 us (4%)
  other arithmetic  2.55 us (2%)
    pallas_call x1, Pallas kernels, deliver(): pl.pallas_call(deliver_kernel, out_shape=(jax.ShapeDtypeStruct((4, 2, 48,...  47.8 us
    pallas_call x1, Pallas kernels, gather(): pl.pallas_call(gather_kernel, out_shape=(jax.ShapeDtypeStruct((SLOTS, HEA...  38.3 us
    pallas_call x1, Pallas kernels, exchange(): pl.pallas_call(exchange_kernel, out_shape=(jax.ShapeDtypeStruct((4, TOK,...  34.4 us
    pallas_call x1, Pallas kernels, attention(): pl.pallas_call(attention_kernel, out_shape=(jax.ShapeDtypeStruct((TOK, QL...  29.6 us
    pallas_call x1, Pallas kernels, combine(): pl.pallas_call(combine_kernel, out_shape=(jax.ShapeDtypeStruct((4 * 96, Q...  4.05 us

profile of v1, /device:TPU:128, one launch (start us, length us, event | category | flops | bytes accessed | tf_op | source)
XLA Modules:
  0.0 165.8 jit_solution(17541013989311948904)
XLA Ops:
  0.6 0.7 fusion.1
  1.3 0.6 stack.2.bounds_ref
  1.9 0.7 slice.4
  2.7 0.1 copy.16
  2.8 1.1 copy.15
  3.8 0.8 pad_maximum_fusion.kv_ref
  4.6 0.3 fusion
  4.9 0.8 pad_maximum_fusion.1
  5.7 1.9 %copy.17 = bf16[1536,128]{1,0:T(8,128)(2,1)} copy(bf16[1536,128]{0,1:T(8,128)(2,1)} %bitcast.19) | data formatting | bytes 786432 | tf_op jit(solution)/shard_map/transpose | solution.py:571
  7.6 38.3 %gather_latents.1 = (bf16[12,8,16,640]{3,2,1,0:T(8,128)(2,1)}, bf16[4,4,96,128]{3,2,1,0:T(8,128)(2,1)}) custom-call(bf16[8,16,640]{2,1,0:T(8,128)(2,1)} %pad_maximum_fusion.kv_ref, bf16[2,8,96,128]{3,2,1,0:T(8,128)(2,1)} %bitcast.21), custom_call_target="tpu_custom_call" | custom-call | tf_op jit(solution)/shard_map/gather_latents/pallas_call | solution.py:170
  46.0 29.6 %attention_backward.1 = (bf16[128,1536]{1,0:T(8,128)(2,1)}, bf16[1536,640]{1,0:T(8,128)(2,1)}, bf16[128,1536]{1,0:T(8,128)(2,1)}) custom-call(bf16[128,1536]{1,0:T(8,128)(2,1)} %bitcast.20, bf16[1536,1536]{1,0:T(8,128)(2,1)} %wq_ref.1, bf16[512,2048]{1,0:T(8,128)(2,1)} %wkv_ref.1, bf16[128,1024]{1,0:T(8,128)(2,1)} %bitcast.26, bf16[1536,640]{1,0:T(8,128)(2,1)} %bitcast.17, ...), custom_call_target="tpu_custom_call" | custom-call | tf_op jit(solution)/shard_map/attention_backward/pallas_call | solution.py:310
  75.6 34.4 %exchange_terms.1 = (bf16[4,128,1536]{2,1,0:T(8,128)(2,1)}, bf16[8,12,16,640]{3,2,1,0:T(8,128)(2,1)}, bf16[8,16,1536]{2,1,0:T(8,128)(2,1)}) custom-call(bf16[128,1536]{1,0:T(8,128)(2,1)} %get-tuple-element.21.dq_ref, bf16[12,8,16,640]{3,2,1,0:T(8,128)(2,1)} %bitcast.18, bf16[8,16,1536]{2,1,0:T(8,128)(2,1)} %bitcast.25), custom_call_target="tpu_custom_call" | custom-call | tf_op jit(solution)/shard_map/exchange_terms/pallas_call | solution.py:376
  110.0 4.0 %combine_terms.1 = (bf16[384,1536]{1,0:T(8,128)(2,1)}, bf16[12,16,640]{2,1,0:T(8,128)(2,1)}, bf16[16,1536]{1,0:T(8,128)(2,1)}) custom-call(bf16[4,4,96,128]{3,2,1,0:T(8,128)(2,1)} %get-tuple-element.19.xg_ref, bf16[4,128,1536]{2,1,0:T(8,128)(2,1)} %get-tuple-element.24.dg_ref, bf16[8,12,16,640]{3,2,1,0:T(8,128)(2,1)} %get-tuple-element.25.rl_ref, ...), custom_call_target="tpu_custom_call" | custom-call | tf_op jit(solution)/shard_map/combine_terms/pallas_call | solution.py:407
  114.0 47.8 %deliver_sums.1 = (bf16[4,2,48,1536]{3,2,1,0:T(8,128)(2,1)}, bf16[12,16,640]{2,1,0:T(8,128)(2,1)}, bf16[8,16,1536]{2,1,0:T(8,128)(2,1)}) custom-call(bf16[4,2,48,1536]{3,2,1,0:T(8,128)(2,1)} %bitcast.22, bf16[12,16,640]{2,1,0:T(8,128)(2,1)} %get-tuple-element.28.ls_ref, bf16[16,1536]{1,0:T(8,128)(2,1)} %get-tuple-element.29.qs_ref), custom_call_target="tpu_custom_call" | custom-call | tf_op jit(solution)/shard_map/deliver_sums/pallas_call | solution.py:515
  161.9 2.1 %finish_sums.1 = (bf16[48,1536]{1,0:T(8,128)(2,1)}, bf16[16,576]{1,0:T(8,128)(2,1)}) custom-call(bf16[4,2,48,1536]{3,2,1,0:T(8,128)(2,1)} %get-tuple-element.31.rw_ref, bf16[12,16,640]{2,1,0:T(8,128)(2,1)} %get-tuple-element.32.rl_ref, s32[1]{0:T(128)} %bitcast.13.count_ref), custom_call_target="tpu_custom_call" | custom-call | tf_op jit(solution)/shard_map/finish_sums/pallas_call | solution.py:545
  164.0 1.8 %copy.20 = bf16[1,128,1536]{2,1,0:T(8,128)(2,1)} copy(bf16[1,128,1536]{2,1,0:T(8,128)(2,1)} %bitcast.24) | data formatting | bytes 786432
  (1 shorter events, 0.0 us)

commit v2 on v0

v2 whole, which is shorter than its diff:
```python
import jax
import jax.numpy as jnp
from jax import lax
from jax.experimental import pallas as pl
from jax.experimental.pallas import tpu as pltpu
from jax.sharding import PartitionSpec as P

QL = 1536
KVL = 512
ROPE = 64
NOPE = 128
VD = 128
HEADS = 8
TOK = 128
SLOTS = 12
SUB = 16
LAT = 640
KEYS = SLOTS * TOK
FIRST = 12
BF = jnp.bfloat16
F32 = jnp.float32
MESH = pl.DeviceIdType.MESH
VMEM_LIMIT = 63 * 1024 * 1024


def place():
    return lax.axis_index("rep"), lax.axis_index("seq"), lax.axis_index("head")


def group_base(s):
    return jnp.where(s < FIRST, 0, FIRST)


def z_partner(s):
    return s + 2 - 4 * lax.rem(lax.div(s, 2), 2)


def peer_rows(s):
    return lax.rem(lax.div(s, 2), 2)


def covered(z, zb, j):
    return lax.rem(jnp.where(zb == 0, z - j + 8, z + j), 8)


def remote(src, dst, send, recv, device):
    return pltpu.make_async_remote_copy(
        src_ref=src, dst_ref=dst, send_sem=send, recv_sem=recv, device_id=device, device_id_type=MESH
    )


def source_z(z, j):
    down = lax.rem(z + j, 8)
    up = lax.rem(z - j + 8, 8)
    return jnp.where(lax.rem(down, 2) == 0, down, up)


NT = (((1,), (1,)), ((), ()))
TN = (((0,), (0,)), ((), ()))
NN = (((1,), (0,)), ((), ()))
PAIRS = HEADS // 2
PARTS = 3
CHUNK = KEYS // PARTS
ROWS = 128


def dot(a, b, dims):
    return lax.dot_general(a, b, dims, preferred_element_type=F32)


def swap_halves(v):
    lane = lax.broadcasted_iota(jnp.int32, v.shape, 1)
    half = ROPE // 2
    return jnp.where(lax.rem(lane, ROPE) < half, pltpu.roll(v, TOK - half, 1), pltpu.roll(v, half, 1))


PIECES = [(j, y) for j in range(4) for y in range(2)]
TURNS = ((1, 0), (0, 1), (1, 1))


def kernel(
    x_ref, kv_ref, wq_hbm, wkv_hbm, do_ref, trig_ref, pos_ref,
    qg_ref, w_ref, l_ref,
    wq_v, wkv_v, kvx_s, xt_s, lat_s, xg_s, a_s, r_s, kvd_s, sp_s, sr_s, dp_s, rope_s, acc_s,
    dg_s, wp_s, rw_s, qt_s, rq_s, qs_s, dl_s, rl_s, ls_s, rlat_s,
    load, s1, r1, s2, r2, sx, rx, sdq, rdq, sw, rw, sqt, rqt, sqa, rqa, sdl, rdl, sls, rls,
):
    r, s, h = place()
    big = s < FIRST
    base = group_base(s)
    slot = s - base
    members = jnp.where(big, SLOTS, 4)
    part = lax.div(slot, 4)
    parts = part + 1
    z, zb, yh = lax.div(s, 2), peer_rows(s), lax.rem(s, 2)
    other = z_partner(s)
    mine = 2 * r + zb
    sibling, partner, diagonal = (1 - r, s, h), (r, other, h), (1 - r, other, h)
    plane = [lax.rem(h + d, HEADS) for d in range(1, HEADS)]
    owners = [(r, 2 * covered(z, zb, j) + lax.rem(yh + y, 2), h) for j, y in PIECES]
    sources = [(r, 2 * source_z(z, j) + lax.rem(yh + y, 2), h) for j, y in PIECES]

    barrier = pltpu.get_barrier_semaphore()

    def signal(device):
        pl.semaphore_signal(barrier, inc=1, device_id=device, device_id_type=MESH)

    for peer in plane:
        signal((r, s, peer))
    for device in (sibling, partner, diagonal):
        signal(device)
    for device in sources[1:]:
        signal(device)
    for k in range(SLOTS):
        @pl.when((k != slot) & (k < members))
        def _():
            signal((r, base + k, h))

    loads = [
        pltpu.make_async_copy(wq_hbm, wq_v, load.at[0]),
        pltpu.make_async_copy(wkv_hbm, wkv_v, load.at[1]),
    ]
    for copy in loads:
        copy.start()
    kvx_s[...] = jnp.concatenate([kv_ref[...], kv_ref[:, KVL:]], 1).reshape(HEADS, SUB, LAT)
    xt_s[...] = x_ref[...].T.reshape(2, 8, 96, TOK)
    lat_s[slot, h] = kvx_s[h]
    pl.semaphore_wait(barrier, members - 1 + 17)

    def to_seq(k):
        return remote(kvx_s.at[h], lat_s.at[slot, h], s1.at[k], r1.at[slot], (r, base + k, h))

    def from_seq(k):
        return remote(kvx_s.at[h], lat_s.at[k, h], s1.at[k], r1.at[k], (r, base + k, h))

    def fresh(k):
        return (k != slot) & (k < members) & (k // 4 >= part)

    def older(k):
        return (k != slot) & (k < members) & (k // 4 <= part)

    for k in range(SLOTS):
        @pl.when(fresh(k))
        def _():
            to_seq(k).start()

    def columns(k, dr, dz, j):
        pr, pzb = lax.rem(r + dr, 2), lax.rem(zb + dz, 2)
        ps = other if dz else s
        return remote(
            xt_s.at[pr, covered(lax.div(ps, 2), pzb, j)], xg_s.at[mine, j], sx.at[k, j], rx.at[k, j], (pr, ps, h)
        )

    for k, (dr, dz) in enumerate(TURNS):
        for j in range(4):
            columns(k, dr, dz, j).start()
    for j in range(4):
        xg_s[mine, j] = xt_s[r, covered(z, zb, j)]

    def slots_of(p):
        return pl.ds(pl.multiple_of(4 * p, 4), 4)

    def to_plane(p, d):
        return remote(
            lat_s.at[slots_of(p), h], lat_s.at[slots_of(p), h], s2.at[p, d], r2.at[p, d], (r, s, plane[d - 1])
        )

    def from_plane(p, d):
        source = lax.rem(h - d + HEADS, HEADS)
        return remote(
            lat_s.at[slots_of(p), h], lat_s.at[slots_of(p), source], s2.at[p, d], r2.at[p, d], (r, s, source)
        )

    for p in range(PARTS):
        for k in range(4 * p, 4 * p + 4):
            @pl.when(older(k))
            def _():
                from_seq(k).wait_recv()

        @pl.when(p < parts)
        def _():
            for d in range(1, HEADS):
                to_plane(p, d).start()

    scale = (NOPE + ROPE) ** (-0.5)
    cosine = jnp.concatenate([trig_ref[:, : ROPE // 2]] * 4, 1)
    sine = jnp.concatenate([-trig_ref[:, ROPE // 2 :], trig_ref[:, ROPE // 2 :]] * 2, 1)
    left = lax.broadcasted_iota(jnp.int32, (TOK, TOK), 1) < ROPE
    loads[0].wait()
    for g in range(PAIRS):
        projected = dot(x_ref[...], wq_v[:, 384 * g : 384 * (g + 1)], NN)
        one, mid, last = (projected[:, TOK * k : TOK * (k + 1)] for k in range(3))
        two = jnp.where(left, pltpu.roll(mid, ROPE, 1), pltpu.roll(last, ROPE, 1))
        none = jnp.zeros((TOK, TOK), BF)
        for k, nope in enumerate((one, two)):
            i = 2 * g + k
            a_s[i, :TOK, :TOK] = nope.astype(BF)
            a_s[i, :TOK, TOK:] = none
            a_s[i, TOK:, :TOK] = none
            a_s[i, TOK:, TOK:] = do_ref[:, TOK * i : TOK * (i + 1)]
        r_s[g, :TOK, :] = jnp.where(left, mid * cosine + swap_halves(mid) * sine, 0.0).astype(BF)
        r_s[g, TOK:, :] = jnp.where(left, 0.0, last * cosine + swap_halves(last) * sine).astype(BF)
    rope_s[...] = jnp.zeros_like(rope_s)
    loads[1].wait()

    def chunk_at(p):
        return pl.ds(pl.multiple_of(p * CHUNK, CHUNK), CHUNK)

    def latent_chunk(p):
        return lat_s[slots_of(p)].reshape(CHUNK, LAT)

    def keys_of(p, nothing):
        for d in range(1, HEADS):
            from_plane(p, d).wait_recv()
        rows = latent_chunk(p)[:, :KVL]
        for g in range(PAIRS):
            kvd_s[g, chunk_at(p), :] = dot(rows, wkv_v[:, 512 * g : 512 * (g + 1)], NN).astype(BF)
        return nothing

    lax.fori_loop(0, parts, keys_of, 0)
    for k, (dr, dz) in enumerate(TURNS):
        source = 2 * lax.rem(r + dr, 2) + lax.rem(zb + dz, 2)
        for j in range(4):
            remote(xt_s.at[0, 0], xg_s.at[source, j], sx.at[k, j], rx.at[k, j], sibling).wait_recv()

    first_row = pl.ds(pl.multiple_of(s * TOK, TOK), TOK)
    high = slot * TOK + lax.broadcasted_iota(jnp.int32, (1, TOK), 1)
    low = high - pos_ref[:, first_row]
    steps = parts * (CHUNK // ROWS)
    fold = (ROWS // 8, 8, TOK)
    both = range(2)

    def hand_out(g, k):
        source = mine if k < 2 else 2 * r + 1 - zb
        return remote(dg_s.at[g, source], dg_s.at[g, source], sdq.at[g, k], rdq.at[g, k], partner if k == 1 else sibling)

    def hand_in(g, k):
        source = (2 * (1 - r) + zb, 2 * r + 1 - zb, 2 * (1 - r) + 1 - zb)[k]
        return remote(dg_s.at[g, source], dg_s.at[g, source], sdq.at[g, k], rdq.at[g, k], sibling)

    def relay(g):
        hand_in(g, 1).wait_recv()
        hand_out(g, 2).start()

    def to_owner(g, n):
        j, y = PIECES[n]
        return remote(
            wp_s.at[g, j, lax.rem(yh + y, 2)], rw_s.at[g, j, y], sw.at[g, n], rw.at[g, n], owners[n]
        )

    def from_source(g, n):
        j, y = PIECES[n]
        return remote(wp_s.at[g, j, y], rw_s.at[g, j, y], sw.at[g, n], rw.at[g, n], sources[n])

    def weights(g):
        hand_in(g, 0).wait_recv()
        hand_in(g, 2).wait_recv()
        rows = jnp.concatenate([xg_s[k].reshape(4 * 96, TOK) for k in range(4)], 1)
        product = dot(rows, dg_s[g].reshape(4 * TOK, 384), NN)
        wp_s[g] = product.astype(BF).reshape(4, 2, 48, 384)
        for n in range(1, 8):
            to_owner(g, n).start()

    def pair(g, carry):
        def scores(p, nothing):
            at = chunk_at(p)
            for k in both:
                sp_s[k, at, :] = dot(kvd_s[g, at, 256 * k : 256 * (k + 1)], a_s[2 * g + k], NT)
            sr_s[at, :] = dot(latent_chunk(p)[:, KVL:], r_s[g], NT)
            return nothing

        lax.fori_loop(0, parts, scores, 0)

        def first(c, tops):
            at = pl.ds(pl.multiple_of(c * ROWS, ROWS), ROWS)
            key = c * ROWS + lax.broadcasted_iota(jnp.int32, (ROWS, TOK), 0)
            seen = (key >= low) & (key <= high)
            out = []
            for k in both:
                value = (sp_s[k, at, :TOK] + sr_s[at, TOK * k : TOK * (k + 1)]) * scale
                value = jnp.where(seen, value, -jnp.inf)
                sp_s[k, at, :TOK] = value
                out.append(jnp.maximum(tops[k], jnp.max(value.reshape(fold), 0)))
            return tuple(out)

        start = jnp.full((8, TOK), -jnp.inf, F32)
        tops = lax.fori_loop(0, steps, first, (start, start))
        tops = [jnp.max(top, 0, keepdims=True) for top in tops]

        def second(c, sums):
            at = pl.ds(pl.multiple_of(c * ROWS, ROWS), ROWS)
            out = []
            for k in both:
                value = jnp.exp(sp_s[k, at, :TOK] - tops[k])
                sp_s[k, at, :TOK] = value
                out.append(sums[2 * k] + jnp.sum(value.reshape(fold), 0))
                out.append(sums[2 * k + 1] + jnp.sum((value * sp_s[k, at, TOK:]).reshape(fold), 0))
            return tuple(out)

        zero = jnp.zeros((8, TOK), F32)
        sums = lax.fori_loop(0, steps, second, (zero,) * 4)
        inverse = [1.0 / jnp.sum(sums[2 * k], 0, keepdims=True) for k in both]
        inner = [jnp.sum(sums[2 * k + 1], 0, keepdims=True) * inverse[k] for k in both]

        @pl.when(g >= 1)
        def _():
            relay(g - 1)

        def third(c, nothing):
            at = pl.ds(pl.multiple_of(c * ROWS, ROWS), ROWS)
            for k in both:
                weight = sp_s[k, at, :TOK] * inverse[k]
                dp_s[k, at, TOK:] = weight.astype(BF)
                dp_s[k, at, :TOK] = (weight * (sp_s[k, at, TOK:] - inner[k]) * scale).astype(BF)
            return nothing

        lax.fori_loop(0, steps, third, 0)
        acc_s[...] = jnp.zeros_like(acc_s)

        def backward(p, nothing):
            at = chunk_at(p)
            key_rope = latent_chunk(p)[:, KVL:]
            for k in both:
                score_grad = dp_s[k, at, :TOK]
                rows = jnp.concatenate([kvd_s[g, at, 256 * k : 256 * k + NOPE], key_rope], 1)
                acc_s[k] += dot(score_grad, rows, TN)
                kvd_s[g, at, 256 * k : 256 * (k + 1)] = dot(dp_s[k, at, :], a_s[2 * g + k], NN).astype(BF)
            grads = jnp.concatenate([dp_s[0, at, :TOK], dp_s[1, at, :TOK]], 1)
            rope_s[at, :] += dot(grads, r_s[g], NN).astype(BF).astype(F32)
            return nothing

        lax.fori_loop(0, parts, backward, 0)
        ropes = []
        for k in both:
            chunk = acc_s[k, :, TOK:]
            ropes.append(chunk * cosine - swap_halves(chunk) * sine)
        second_nope = pltpu.roll(acc_s[1, :, :TOK], ROPE, 1)
        dg_s[g, mine] = jnp.concatenate(
            [acc_s[0, :, :TOK], jnp.where(left, ropes[0], second_nope), jnp.where(left, second_nope, ropes[1])], 1
        ).astype(BF)
        hand_out(g, 0).start()
        hand_out(g, 1).start()

        @pl.when(g >= 1)
        def _():
            weights(g - 1)

        return carry

    lax.fori_loop(0, PAIRS, pair, 0)

    joined = jnp.concatenate([dg_s[g, mine] for g in range(PAIRS)], 1)
    qt_s[...] = dot(joined, wq_v[...], NT).astype(BF).reshape(HEADS, SUB, QL)

    def query_out(d):
        return remote(qt_s.at[plane[d - 1]], rq_s.at[h], sqt.at[d], rqt.at[d], (r, s, plane[d - 1]))

    for d in range(1, HEADS):
        query_out(d).start()
    relay(PAIRS - 1)

    def latent_out(p, d):
        return remote(
            dl_s.at[slots_of(p), plane[d - 1]], rl_s.at[h, slots_of(p)], sdl.at[p, d], rdl.at[p, d],
            (r, s, plane[d - 1]),
        )

    def latent_in(p, d):
        source = lax.rem(h - d + HEADS, HEADS)
        return remote(
            dl_s.at[slots_of(p), h], rl_s.at[source, slots_of(p)], sdl.at[p, d], rdl.at[p, d], (r, s, source)
        )

    def latents(p, nothing):
        at = chunk_at(p)
        rows = jnp.concatenate([kvd_s[g, at, :] for g in range(PAIRS)], 1)
        low_part = dot(rows, wkv_v[...], NT).astype(BF)
        rope = rope_s[at, :]
        rope = (rope + pltpu.roll(rope, ROPE, 1)).astype(BF)
        dl_s[slots_of(p)] = jnp.concatenate([low_part, rope], 1).reshape(4, HEADS, SUB, LAT)
        for d in range(1, HEADS):
            latent_out(p, d).start()
        return nothing

    lax.fori_loop(0, parts, latents, 0)
    weights(PAIRS - 1)

    total = qt_s[h].astype(F32)
    for d in range(1, HEADS):
        source = lax.rem(h - d + HEADS, HEADS)
        remote(qt_s.at[h], rq_s.at[source], sqt.at[d], rqt.at[d], (r, s, source)).wait_recv()
        total += rq_s[source].astype(F32)
    qs_s[...] = total.astype(BF)
    qg_ref[h] = qs_s[...]

    def query_share(d):
        return remote(qs_s, qg_ref.at[h], sqa.at[d], rqa.at[d], (r, s, plane[d - 1]))

    for d in range(1, HEADS):
        query_share(d).start()

    def to_latent_owner(k):
        return remote(ls_s.at[k], rlat_s.at[slot], sls.at[k], rls.at[slot], (r, base + k, h))

    def from_latent_source(k):
        return remote(ls_s.at[k], rlat_s.at[k], sls.at[k], rls.at[k], (r, base + k, h))

    for p in range(PARTS):
        @pl.when(p < parts)
        def _():
            for d in range(1, HEADS):
                latent_in(p, d).wait_recv()
            for k in range(4 * p, 4 * p + 4):
                total = dl_s[k, h].astype(F32)
                for d in range(1, HEADS):
                    total += rl_s[lax.rem(h + d, HEADS), k].astype(F32)
                ls_s[k] = total.astype(BF)

                @pl.when(older(k))
                def _():
                    to_latent_owner(k).start()

    for g in range(PAIRS):
        total = wp_s[g, 0, yh].astype(F32)
        for n in range(1, 8):
            from_source(g, n).wait_recv()
            total += rw_s[g, n // 2, n % 2].astype(F32)
        w_ref[:, 384 * g : 384 * (g + 1)] = total.astype(BF)

    acc_s[0, :SUB, :] = ls_s[slot, :, :256].astype(F32)
    acc_s[0, SUB : 2 * SUB, :] = ls_s[slot, :, 256:512].astype(F32)
    acc_s[0, 2 * SUB : 3 * SUB, :TOK] = ls_s[slot, :, 512:].astype(F32)
    for k in range(SLOTS):
        @pl.when(fresh(k))
        def _():
            from_latent_source(k).wait_recv()
            acc_s[0, :SUB, :] += rlat_s[k, :, :256].astype(F32)
            acc_s[0, SUB : 2 * SUB, :] += rlat_s[k, :, 256:512].astype(F32)
            acc_s[0, 2 * SUB : 3 * SUB, :TOK] += rlat_s[k, :, 512:].astype(F32)
    l_ref[...] = jnp.concatenate(
        [acc_s[0, :SUB, :], acc_s[0, SUB : 2 * SUB, :], acc_s[0, 2 * SUB : 3 * SUB, :ROPE]], 1
    ).astype(BF)

    for d in range(1, HEADS):
        source = lax.rem(h - d + HEADS, HEADS)
        remote(qs_s, qg_ref.at[source], sqa.at[d], rqa.at[d], (r, s, source)).wait_recv()
        query_share(d).wait_send()
        query_out(d).wait_send()
    for k in range(SLOTS):
        @pl.when(fresh(k))
        def _():
            to_seq(k).wait_send()

        @pl.when(older(k))
        def _():
            to_latent_owner(k).wait_send()
    for k, (dr, dz) in enumerate(TURNS):
        for j in range(4):
            columns(k, dr, dz, j).wait_send()

    def drain_part(p, nothing):
        for d in range(1, HEADS):
            to_plane(p, d).wait_send()
            latent_out(p, d).wait_send()
        return nothing

    lax.fori_loop(0, parts, drain_part, 0)

    def drain_pair(g, nothing):
        for k in range(3):
            hand_out(g, k).wait_send()
        for n in range(1, 8):
            to_owner(g, n).wait_send()
        return nothing

    lax.fori_loop(0, PAIRS, drain_pair, 0)


def backward_pass(x, kv, wq, wkv, do, trig, positions):
    dma = pltpu.SemaphoreType.DMA
    vmem = pl.BlockSpec(memory_space=pltpu.VMEM)
    hbm = pl.BlockSpec(memory_space=pl.ANY)
    return pl.pallas_call(
        kernel,
        out_shape=(
            jax.ShapeDtypeStruct((HEADS, SUB, QL), BF),
            jax.ShapeDtypeStruct((48, QL), BF),
            jax.ShapeDtypeStruct((SUB, KVL + ROPE), BF),
        ),
        in_specs=[vmem, vmem, hbm, hbm, vmem, vmem, vmem],
        out_specs=(vmem,) * 3,
        scratch_shapes=[
            pltpu.VMEM((QL, QL), BF),
            pltpu.VMEM((KVL, 2048), BF),
            pltpu.VMEM((HEADS, SUB, LAT), BF),
            pltpu.VMEM((2, 8, 96, TOK), BF),
            pltpu.VMEM((SLOTS, HEADS, SUB, LAT), BF),
            pltpu.VMEM((4, 4, 96, TOK), BF),
            pltpu.VMEM((HEADS, 2 * TOK, 2 * TOK), BF),
            pltpu.VMEM((PAIRS, 2 * TOK, TOK), BF),
            pltpu.VMEM((PAIRS, KEYS, 512), BF),
            pltpu.VMEM((2, KEYS, 2 * TOK), F32),
            pltpu.VMEM((KEYS, 2 * TOK), F32),
            pltpu.VMEM((2, KEYS, 2 * TOK), BF),
            pltpu.VMEM((KEYS, TOK), F32),
            pltpu.VMEM((2, TOK, 2 * TOK), F32),
            pltpu.VMEM((PAIRS, 4, TOK, 384), BF),
            pltpu.VMEM((PAIRS, 4, 2, 48, 384), BF),
            pltpu.VMEM((PAIRS, 4, 2, 48, 384), BF),
            pltpu.VMEM((HEADS, SUB, QL), BF),
            pltpu.VMEM((HEADS, SUB, QL), BF),
            pltpu.VMEM((SUB, QL), BF),
            pltpu.VMEM((SLOTS, HEADS, SUB, LAT), BF),
            pltpu.VMEM((HEADS, SLOTS, SUB, LAT), BF),
            pltpu.VMEM((SLOTS, SUB, LAT), BF),
            pltpu.VMEM((SLOTS, SUB, LAT), BF),
            dma((2,)),
            dma((SLOTS,)), dma((SLOTS,)),
            dma((PARTS, HEADS)), dma((PARTS, HEADS)),
            dma((3, 4)), dma((3, 4)),
            dma((PAIRS, 3)), dma((PAIRS, 3)),
            dma((PAIRS, 8)), dma((PAIRS, 8)),
            dma((HEADS,)), dma((HEADS,)),
            dma((HEADS,)), dma((HEADS,)),
            dma((PARTS, HEADS)), dma((PARTS, HEADS)),
            dma((SLOTS,)), dma((SLOTS,)),
        ],
        compiler_params=pltpu.CompilerParams(
            collective_id=0, has_side_effects=True, vmem_limit_bytes=VMEM_LIMIT
        ),
        name="attention_backward",
    )(x, kv, wq, wkv, do, trig, positions)


def shards(query_latent, kv_latent, query_up, kv_up, out_grad, positions):
    s = lax.axis_index("seq")
    local_positions = lax.dynamic_slice_in_dim(positions[0], s * TOK, TOK)
    half = ROPE // 2
    rates = 10000.0 ** (-jnp.arange(half, dtype=F32) / half)
    angles = local_positions.astype(F32)[:, None] * rates[None, :]
    trig = jnp.concatenate([jnp.cos(angles), jnp.sin(angles)], 1)
    query_grad, weight_grad, latent_grad = backward_pass(
        query_latent[0], kv_latent[0], query_up, kv_up, out_grad[0], trig, positions
    )
    return query_grad.reshape(1, TOK, QL), latent_grad[None], weight_grad


def solution(mesh):
    return jax.shard_map(
        shards,
        mesh=mesh,
        in_specs=(
            P("rep", "seq", None),
            P("rep", "seq", None),
            P(None, "head"),
            P(None, "head"),
            P("rep", "seq", "head"),
            P("rep", None),
        ),
        out_specs=(
            P("rep", "seq", None),
            P("rep", ("seq", "head"), None),
            P(("rep", "seq"), "head"),
        ),
        check_vma=False,
    )
```

time: 1040 us -> 116 us (0.11)
  waiting for transfers between devices: 869 us -> 0 us
  Pallas kernels: 0 us -> 107 us
  matrix products: 66.8 us -> 0 us
  blocking collectives: 41.6 us -> 0 us
  local copies, waits for them, and re-layouts: 31.3 us -> 6.39 us
  between operations: 14 us -> 0.65 us
  other arithmetic: 13.5 us -> 1.7 us
    unnamed x4 -> x0, waiting for transfers between devices: 635 us -> none
    reduce_scatter x1 -> x0, waiting for transfers between devices: 157 us -> none  [shards(): lax.psum_scatter(weight_term, ('rep', 'seq'), scatter_dimension=0, tiled=...]
    pallas_call x0 -> x1, Pallas kernels: none -> 107 us  [backward_pass(): pl.pallas_call(kernel, out_shape=(jax.ShapeDtypeStruct((HEADS, SUB, QL),...]
    all_gather x1 -> x0, waiting for transfers between devices: 76.3 us -> none  [shards(): shard_rows = lax.all_gather(kv_latent[0], 'seq', axis=0, tiled=True)]
    dot_general x10 -> x0, matrix products: 66.8 us -> none  [the longest x1 15.9 us: shards(): jnp.einsum('hqk,hqd->hkd', score_grad, queries, preferred_element_type=jn...]
    psum x1 -> x0, blocking collectives: 41.6 us -> none  [shards(): query_grad = lax.psum(query_term, 'head').astype(jnp.bfloat16)[None]]
    unnamed x17 -> x4, local copies, waits for them, and re-layouts: 17.8 us -> 6.39 us
  transfers between devices with their start and end apart: 3 -> 0, of which waited for: 3 -> 0; matrix products, arithmetic and copies ran while one was open for 5% -> 0% of each run, Pallas kernels for 0% -> 0%
where the time goes in v2:
time: 116 us
  Pallas kernels  107 us (92%)
  local copies, waits for them, and re-layouts  6.39 us (6%)
  other arithmetic  1.7 us (1%)
    pallas_call x1, Pallas kernels, backward_pass(): pl.pallas_call(kernel, out_shape=(jax.ShapeDtypeStruct((HEADS, SUB, QL),...  107 us
    unnamed x4, local copies, waits for them, and re-layouts  6.39 us

profile of v2, /device:TPU:128, one launch (start us, length us, event | category | flops | bytes accessed | tf_op | source)
XLA Modules:
  0.0 116.0 jit_solution(4765550342301392723)
XLA Ops:
  0.6 0.7 convert_bitcast_fusion
  1.3 0.3 multiply_cosine_fusion
  1.6 0.7 pad_maximum_fusion.trig_ref
  2.3 1.7 %copy.10 = bf16[1,128,576]{2,1,0:T(8,128)(2,1)} copy(bf16[1,128,576]{1,2,0:T(8,128)(2,1)} %param.7) | data formatting | bytes 294912 | tf_op args[1]
  4.1 107.3 %attention_backward.1 = (bf16[8,16,1536]{2,1,0:T(8,128)(2,1)}, bf16[48,1536]{1,0:T(8,128)(2,1)}, bf16[16,576]{1,0:T(8,128)(2,1)}) custom-call(bf16[128,1536]{1,0:T(8,128)(2,1)} %bitcast.8, bf16[128,576]{1,0:T(8,128)(2,1)} %bitcast.7, bf16[1536,1536]{1,0:T(8,128)(2,1)} %wq_hbm.1, bf16[512,2048]{1,0:T(8,128)(2,1)} %wkv_hbm.1, bf16[128,1024]{1,0:T(8,128)(2,1)} %bitcast.10, ...), custom_call_target="tpu_custom_call" | custom-call | tf_op jit(solution)/shard_map/attention_backward/pallas_call | solution.py:483
  111.3 1.8 %copy.15 = bf16[1,128,1536]{2,1,0:T(8,128)(2,1)} copy(bf16[1,128,1536]{2,1,0:T(8,128)(2,1)} %bitcast.9) | data formatting | bytes 786432
  113.1 1.3 %copy.16 = bf16[1,16,576]{2,1,0:T(8,128)(2,1)} copy(bf16[1,16,576]{2,1,0:T(8,128)(2,1)} %bitcast.11) | data formatting | bytes 36864
  114.4 1.6 %copy.17 = bf16[48,1536]{1,0:T(8,128)(2,1)} copy(bf16[48,1536]{1,0:T(8,128)(2,1)} %get-tuple-element.16) | data formatting | bytes 294912
  (1 shorter events, 0.0 us)

commit v3 on v2

--- a/solution.py
+++ b/solution.py
@@ -39,6 +39,10 @@
     return lax.rem(lax.div(s, 2), 2)
 
 
+def member(r, zb, yh):
+    return 4 * r + 2 * zb + yh
+
+
 def covered(z, zb, j):
     return lax.rem(jnp.where(zb == 0, z - j + 8, z + j), 8)
 
@@ -47,6 +51,10 @@
     return pltpu.make_async_remote_copy(
         src_ref=src, dst_ref=dst, send_sem=send, recv_sem=recv, device_id=device, device_id_type=MESH
     )
+
+
+def window(z, zb):
+    return jnp.where(zb == 0, lax.rem(z + 5, 8), z)
 
 
 def source_z(z, j):
@@ -74,15 +82,16 @@
     return jnp.where(lax.rem(lane, ROPE) < half, pltpu.roll(v, TOK - half, 1), pltpu.roll(v, half, 1))
 
 
-PIECES = [(j, y) for j in range(4) for y in range(2)]
-TURNS = ((1, 0), (0, 1), (1, 1))
+TURNS = [(dr, dz, dy) for dr in range(2) for dz in range(2) for dy in range(2)][1:]
+MEMBERS = 8
+REACH = 4
 
 
 def kernel(
     x_ref, kv_ref, wq_hbm, wkv_hbm, do_ref, trig_ref, pos_ref,
     qg_ref, w_ref, l_ref,
     wq_v, wkv_v, kvx_s, xt_s, lat_s, xg_s, a_s, r_s, kvd_s, sp_s, sr_s, dp_s, rope_s, acc_s,
-    dg_s, wp_s, rw_s, qt_s, rq_s, qs_s, dl_s, rl_s, ls_s, rlat_s,
+    dg_s, wp_s, rw_s, qt_s, rq_s, qs_s, dl_s, rl_s, ts_s, ry_s, ls_s, rlat_s,
     load, s1, r1, s2, r2, sx, rx, sdq, rdq, sw, rw, sqt, rqt, sqa, rqa, sdl, rdl, sls, rls,
 ):
     r, s, h = place()
@@ -94,11 +103,13 @@
     parts = part + 1
     z, zb, yh = lax.div(s, 2), peer_rows(s), lax.rem(s, 2)
     other = z_partner(s)
-    mine = 2 * r + zb
-    sibling, partner, diagonal = (1 - r, s, h), (r, other, h), (1 - r, other, h)
+    mine = member(r, zb, yh)
+    across = lax.rem(yh + 1, 2) - yh
+    sibling, partner, far = (1 - r, s, h), (r, other, h), (r, s + across, h)
     plane = [lax.rem(h + d, HEADS) for d in range(1, HEADS)]
-    owners = [(r, 2 * covered(z, zb, j) + lax.rem(yh + y, 2), h) for j, y in PIECES]
-    sources = [(r, 2 * source_z(z, j) + lax.rem(yh + y, 2), h) for j, y in PIECES]
+    circle = [(lax.rem(r + dr, 2), (other if dz else s) + across * dy, h) for dr, dz, dy in TURNS]
+    owners = [(r, 2 * covered(z, zb, d) + yh, h) for d in range(REACH)]
+    sources = [(r, 2 * source_z(z, d) + yh, h) for d in range(REACH)]
 
     barrier = pltpu.get_barrier_semaphore()
 
@@ -107,7 +118,7 @@
 
     for peer in plane:
         signal((r, s, peer))
-    for device in (sibling, partner, diagonal):
+    for device in circle:
         signal(device)
     for device in sources[1:]:
         signal(device)
@@ -122,8 +133,7 @@
     ]
     for copy in loads:
         copy.start()
-    kvx_s[...] = jnp.concatenate([kv_ref[...], kv_ref[:, KVL:]], 1).reshape(HEADS, SUB, LAT)
-    xt_s[...] = x_ref[...].T.reshape(2, 8, 96, TOK)
+    kvx_s[...] = jnp.concatenate([kv_ref[...], kv_ref[KVL:, :]], 0).T.reshape(HEADS, SUB, LAT)
     lat_s[slot, h] = kvx_s[h]
     pl.semaphore_wait(barrier, members - 1 + 17)
 
@@ -137,25 +147,18 @@
         return (k != slot) & (k < members) & (k // 4 >= part)
 
     def older(k):
-        return (k != slot) & (k < members) & (k // 4 <= part)
+        return (k != slot) & (k < members) & ((k // 4 if isinstance(k, int) else lax.div(k, 4)) <= part)
 
     for k in range(SLOTS):
         @pl.when(fresh(k))
         def _():
             to_seq(k).start()
 
-    def columns(k, dr, dz, j):
-        pr, pzb = lax.rem(r + dr, 2), lax.rem(zb + dz, 2)
-        ps = other if dz else s
-        return remote(
-            xt_s.at[pr, covered(lax.div(ps, 2), pzb, j)], xg_s.at[mine, j], sx.at[k, j], rx.at[k, j], (pr, ps, h)
-        )
-
-    for k, (dr, dz) in enumerate(TURNS):
-        for j in range(4):
-            columns(k, dr, dz, j).start()
-    for j in range(4):
-        xg_s[mine, j] = xt_s[r, covered(z, zb, j)]
+    def columns(k):
+        dr, dz, dy = TURNS[k]
+        pr, pzb, py = lax.rem(r + dr, 2), lax.rem(zb + dz, 2), lax.rem(yh + dy, 2)
+        start = window(lax.div(other if dz else s, 2), pzb)
+        return remote(xt_s.at[pr, pl.ds(start, REACH), py], xg_s.at[mine], sx.at[k], rx.at[k], circle[k])
 
     def slots_of(p):
         return pl.ds(pl.multiple_of(4 * p, 4), 4)
@@ -170,17 +173,6 @@
         return remote(
             lat_s.at[slots_of(p), h], lat_s.at[slots_of(p), source], s2.at[p, d], r2.at[p, d], (r, s, source)
         )
-
-    for p in range(PARTS):
-        for k in range(4 * p, 4 * p + 4):
-            @pl.when(older(k))
-            def _():
-                from_seq(k).wait_recv()
-
-        @pl.when(p < parts)
-        def _():
-            for d in range(1, HEADS):
-                to_plane(p, d).start()
 
     scale = (NOPE + ROPE) ** (-0.5)
     cosine = jnp.concatenate([trig_ref[:, : ROPE // 2]] * 4, 1)
@@ -201,6 +193,23 @@
         r_s[g, :TOK, :] = jnp.where(left, mid * cosine + swap_halves(mid) * sine, 0.0).astype(BF)
         r_s[g, TOK:, :] = jnp.where(left, 0.0, last * cosine + swap_halves(last) * sine).astype(BF)
     rope_s[...] = jnp.zeros_like(rope_s)
+    def share(i, nothing):
+        p = part - i
+        for k in range(4):
+            @pl.when(older(4 * p + k))
+            def _():
+                from_seq(4 * p + k).wait_recv()
+        for d in range(1, HEADS):
+            to_plane(p, d).start()
+        return nothing
+
+    lax.fori_loop(0, parts, share, 0)
+    turned = x_ref[...].T.reshape(2, 8, 2, 48, TOK)
+    xt_s[:, :8] = turned
+    xt_s[:, 8:] = turned
+    for k in range(7):
+        columns(k).start()
+    xg_s[mine] = xt_s[r, pl.ds(window(z, zb), REACH), yh]
     loads[1].wait()
 
     def chunk_at(p):
@@ -209,7 +218,8 @@
     def latent_chunk(p):
         return lat_s[slots_of(p)].reshape(CHUNK, LAT)
 
-    def keys_of(p, nothing):
+    def keys_of(i, nothing):
+        p = part - i
         for d in range(1, HEADS):
             from_plane(p, d).wait_recv()
         rows = latent_chunk(p)[:, :KVL]
@@ -218,11 +228,6 @@
         return nothing
 
     lax.fori_loop(0, parts, keys_of, 0)
-    for k, (dr, dz) in enumerate(TURNS):
-        source = 2 * lax.rem(r + dr, 2) + lax.rem(zb + dz, 2)
-        for j in range(4):
-            remote(xt_s.at[0, 0], xg_s.at[source, j], sx.at[k, j], rx.at[k, j], sibling).wait_recv()
-
     first_row = pl.ds(pl.multiple_of(s * TOK, TOK), TOK)
     high = slot * TOK + lax.broadcasted_iota(jnp.int32, (1, TOK), 1)
     low = high - pos_ref[:, first_row]
@@ -230,36 +235,54 @@
     fold = (ROWS // 8, 8, TOK)
     both = range(2)
 
+    routes = [
+        (0, 0, sibling), (0, 0, partner), (0, 0, far), (1, 0, sibling), (1, 0, far), (0, 1, sibling), (1, 1, sibling)
+    ]
+    arrivals = [(1, 0, 0), (0, 1, 0), (0, 0, 1), (1, 1, 0), (0, 1, 1), (1, 0, 1), (1, 1, 1)]
+
+    def turn(dr, dz, dy):
+        return member(lax.rem(r + dr, 2), lax.rem(zb + dz, 2), lax.rem(yh + dy, 2))
+
     def hand_out(g, k):
-        source = mine if k < 2 else 2 * r + 1 - zb
-        return remote(dg_s.at[g, source], dg_s.at[g, source], sdq.at[g, k], rdq.at[g, k], partner if k == 1 else sibling)
+        dz, dy, device = routes[k]
+        block = dg_s.at[g, turn(0, dz, dy)]
+        return remote(block, block, sdq.at[g, k], rdq.at[g, k], device)
 
     def hand_in(g, k):
-        source = (2 * (1 - r) + zb, 2 * r + 1 - zb, 2 * (1 - r) + 1 - zb)[k]
-        return remote(dg_s.at[g, source], dg_s.at[g, source], sdq.at[g, k], rdq.at[g, k], sibling)
-
-    def relay(g):
-        hand_in(g, 1).wait_recv()
-        hand_out(g, 2).start()
-
-    def to_owner(g, n):
-        j, y = PIECES[n]
-        return remote(
-            wp_s.at[g, j, lax.rem(yh + y, 2)], rw_s.at[g, j, y], sw.at[g, n], rw.at[g, n], owners[n]
-        )
-
-    def from_source(g, n):
-        j, y = PIECES[n]
-        return remote(wp_s.at[g, j, y], rw_s.at[g, j, y], sw.at[g, n], rw.at[g, n], sources[n])
+        block = dg_s.at[g, turn(*arrivals[k])]
+        return remote(block, block, sdq.at[g, k], rdq.at[g, k], sibling)
+
+    def relay(g, arrived, onward):
+        hand_in(g, arrived).wait_recv()
+        for k in onward:
+            hand_out(g, k).start()
+
+    def relay_z(g):
+        relay(g, 1, (4, 3))
+
+    def relay_y(g):
+        relay(g, 2, (5,))
+
+    def relay_zy(g):
+        relay(g, 4, (6,))
+
+    def piece(d):
+        return jnp.where(zb == 0, REACH - 1 - d, d)
+
+    def to_owner(g, d):
+        return remote(wp_s.at[g, piece(d)], rw_s.at[g, d], sw.at[g, d], rw.at[g, d], owners[d])
+
+    def from_source(g, d):
+        return remote(wp_s.at[g, 0], rw_s.at[g, d], sw.at[g, d], rw.at[g, d], sources[d])
 
     def weights(g):
-        hand_in(g, 0).wait_recv()
-        hand_in(g, 2).wait_recv()
-        rows = jnp.concatenate([xg_s[k].reshape(4 * 96, TOK) for k in range(4)], 1)
-        product = dot(rows, dg_s[g].reshape(4 * TOK, 384), NN)
-        wp_s[g] = product.astype(BF).reshape(4, 2, 48, 384)
-        for n in range(1, 8):
-            to_owner(g, n).start()
+        for k in (0, 3, 5, 6):
+            hand_in(g, k).wait_recv()
+        rows = jnp.concatenate([xg_s[k].reshape(REACH * 48, TOK) for k in range(MEMBERS)], 1)
+        product = dot(rows, dg_s[g].reshape(MEMBERS * TOK, 384), NN)
+        wp_s[g] = product.astype(BF).reshape(REACH, 48, 384)
+        for d in (3, 2, 1):
+            to_owner(g, d).start()
 
     def pair(g, carry):
         def scores(p, nothing):
@@ -304,7 +327,11 @@
 
         @pl.when(g >= 1)
         def _():
-            relay(g - 1)
+            relay_z(g - 1)
+
+        @pl.when(g >= 2)
+        def _():
+            relay_zy(g - 2)
 
         def third(c, nothing):
             at = pl.ds(pl.multiple_of(c * ROWS, ROWS), ROWS)
@@ -338,12 +365,21 @@
         dg_s[g, mine] = jnp.concatenate(
             [acc_s[0, :, :TOK], jnp.where(left, ropes[0], second_nope), jnp.where(left, second_nope, ropes[1])], 1
         ).astype(BF)
-        hand_out(g, 0).start()
-        hand_out(g, 1).start()
+        for k in (1, 2, 0):
+            hand_out(g, k).start()
 
         @pl.when(g >= 1)
         def _():
-            weights(g - 1)
+            relay_y(g - 1)
+
+        @pl.when(g == 2)
+        def _():
+            for k, (dr, dz, dy) in enumerate(TURNS):
+                remote(xg_s.at[mine], xg_s.at[turn(dr, dz, dy)], sx.at[k], rx.at[k], sibling).wait_recv()
+
+        @pl.when(g >= 2)
+        def _():
+            weights(g - 2)
 
         return carry
 
@@ -357,32 +393,55 @@
 
     for d in range(1, HEADS):
         query_out(d).start()
-    relay(PAIRS - 1)
+
+    row, column = lax.div(h, 4), lax.rem(h, 4)
 
     def latent_out(p, d):
+        to = lax.rem(column + d, 4)
         return remote(
-            dl_s.at[slots_of(p), plane[d - 1]], rl_s.at[h, slots_of(p)], sdl.at[p, d], rdl.at[p, d],
-            (r, s, plane[d - 1]),
+            dl_s.at[slots_of(p), :, to], rl_s.at[column, slots_of(p)], sdl.at[p, d], rdl.at[p, d],
+            (r, s, 4 * row + to),
         )
 
     def latent_in(p, d):
-        source = lax.rem(h - d + HEADS, HEADS)
+        source = lax.rem(column - d + 4, 4)
         return remote(
-            dl_s.at[slots_of(p), h], rl_s.at[source, slots_of(p)], sdl.at[p, d], rdl.at[p, d], (r, s, source)
+            dl_s.at[slots_of(p), :, column], rl_s.at[source, slots_of(p)], sdl.at[p, d], rdl.at[p, d],
+            (r, s, 4 * row + source),
         )
 
-    def latents(p, nothing):
+    def latent_cross(p):
+        return remote(
+            ts_s.at[slots_of(p), 1 - row], ry_s.at[slots_of(p)], sdl.at[p, 0], rdl.at[p, 0],
+            (r, s, 4 * (1 - row) + column),
+        )
+
+    def latents(p):
         at = chunk_at(p)
         rows = jnp.concatenate([kvd_s[g, at, :] for g in range(PAIRS)], 1)
         low_part = dot(rows, wkv_v[...], NT).astype(BF)
         rope = rope_s[at, :]
         rope = (rope + pltpu.roll(rope, ROPE, 1)).astype(BF)
-        dl_s[slots_of(p)] = jnp.concatenate([low_part, rope], 1).reshape(4, HEADS, SUB, LAT)
-        for d in range(1, HEADS):
+        dl_s[slots_of(p)] = jnp.concatenate([low_part, rope], 1).reshape(4, 2, 4, SUB, LAT)
+        for d in range(1, 4):
             latent_out(p, d).start()
-        return nothing
-
-    lax.fori_loop(0, parts, latents, 0)
+
+    latents(0)
+    relay_z(PAIRS - 1)
+    relay_zy(PAIRS - 2)
+
+    @pl.when(parts > 1)
+    def _():
+        latents(1)
+
+    relay_y(PAIRS - 1)
+    weights(PAIRS - 2)
+
+    @pl.when(parts > 2)
+    def _():
+        latents(2)
+
+    relay_zy(PAIRS - 1)
     weights(PAIRS - 1)
 
     total = qt_s[h].astype(F32)
@@ -405,26 +464,40 @@
     def from_latent_source(k):
         return remote(ls_s.at[k], rlat_s.at[k], sls.at[k], rls.at[k], (r, base + k, h))
 
-    for p in range(PARTS):
+    def add_row(p):
+        for d in range(1, 4):
+            latent_in(p, d).wait_recv()
+        for k in range(4 * p, 4 * p + 4):
+            total = dl_s[k, :, column].astype(F32)
+            for d in range(1, 4):
+                total += rl_s[lax.rem(column + d, 4), k].astype(F32)
+            ts_s[k] = total.astype(BF)
+        latent_cross(p).start()
+
+    def add_column(p):
+        latent_cross(p).wait_recv()
+        for k in range(4 * p, 4 * p + 4):
+            ls_s[k] = (ts_s[k, row].astype(F32) + ry_s[k].astype(F32)).astype(BF)
+
+            @pl.when(older(k))
+            def _():
+                to_latent_owner(k).start()
+
+    add_row(0)
+    for p in range(1, PARTS):
         @pl.when(p < parts)
         def _():
-            for d in range(1, HEADS):
-                latent_in(p, d).wait_recv()
-            for k in range(4 * p, 4 * p + 4):
-                total = dl_s[k, h].astype(F32)
-                for d in range(1, HEADS):
-                    total += rl_s[lax.rem(h + d, HEADS), k].astype(F32)
-                ls_s[k] = total.astype(BF)
-
-                @pl.when(older(k))
-                def _():
-                    to_latent_owner(k).start()
+            add_row(p)
+
+        add_column(p - 1) if p == 1 else pl.when(p - 1 < parts)(lambda: add_column(p - 1))
+
+    pl.when(PARTS - 1 < parts)(lambda: add_column(PARTS - 1))
 
     for g in range(PAIRS):
-        total = wp_s[g, 0, yh].astype(F32)
-        for n in range(1, 8):
-            from_source(g, n).wait_recv()
-            total += rw_s[g, n // 2, n % 2].astype(F32)
+        total = wp_s[g, piece(0)].astype(F32)
+        for d in range(1, REACH):
+            from_source(g, d).wait_recv()
+            total += rw_s[g, d].astype(F32)
         w_ref[:, 384 * g : 384 * (g + 1)] = total.astype(BF)
 
     acc_s[0, :SUB, :] = ls_s[slot, :, :256].astype(F32)
@@ -454,23 +527,24 @@
         @pl.when(older(k))
         def _():
             to_latent_owner(k).wait_send()
-    for k, (dr, dz) in enumerate(TURNS):
-        for j in range(4):
-            columns(k, dr, dz, j).wait_send()
+    for k in range(7):
+        columns(k).wait_send()
 
     def drain_part(p, nothing):
         for d in range(1, HEADS):
             to_plane(p, d).wait_send()
+        for d in range(1, 4):
             latent_out(p, d).wait_send()
+        latent_cross(p).wait_send()
         return nothing
 
     lax.fori_loop(0, parts, drain_part, 0)
 
     def drain_pair(g, nothing):
-        for k in range(3):
+        for k in range(7):
             hand_out(g, k).wait_send()
-        for n in range(1, 8):
-            to_owner(g, n).wait_send()
+        for d in range(1, REACH):
+            to_owner(g, d).wait_send()
         return nothing
 
     lax.fori_loop(0, PAIRS, drain_pair, 0)
@@ -493,9 +567,9 @@
             pltpu.VMEM((QL, QL), BF),
             pltpu.VMEM((KVL, 2048), BF),
             pltpu.VMEM((HEADS, SUB, LAT), BF),
-            pltpu.VMEM((2, 8, 96, TOK), BF),
+            pltpu.VMEM((2, 16, 2, 48, TOK), BF),
             pltpu.VMEM((SLOTS, HEADS, SUB, LAT), BF),
-            pltpu.VMEM((4, 4, 96, TOK), BF),
+            pltpu.VMEM((MEMBERS, REACH, 48, TOK), BF),
             pltpu.VMEM((HEADS, 2 * TOK, 2 * TOK), BF),
             pltpu.VMEM((PAIRS, 2 * TOK, TOK), BF),
             pltpu.VMEM((PAIRS, KEYS, 512), BF),
@@ -504,22 +578,24 @@
             pltpu.VMEM((2, KEYS, 2 * TOK), BF),
             pltpu.VMEM((KEYS, TOK), F32),
             pltpu.VMEM((2, TOK, 2 * TOK), F32),
-            pltpu.VMEM((PAIRS, 4, TOK, 384), BF),
-            pltpu.VMEM((PAIRS, 4, 2, 48, 384), BF),
-            pltpu.VMEM((PAIRS, 4, 2, 48, 384), BF),
+            pltpu.VMEM((PAIRS, MEMBERS, TOK, 384), BF),
+            pltpu.VMEM((PAIRS, REACH, 48, 384), BF),
+            pltpu.VMEM((PAIRS, REACH, 48, 384), BF),
             pltpu.VMEM((HEADS, SUB, QL), BF),
             pltpu.VMEM((HEADS, SUB, QL), BF),
             pltpu.VMEM((SUB, QL), BF),
-            pltpu.VMEM((SLOTS, HEADS, SUB, LAT), BF),
-            pltpu.VMEM((HEADS, SLOTS, SUB, LAT), BF),
+            pltpu.VMEM((SLOTS, 2, 4, SUB, LAT), BF),
+            pltpu.VMEM((4, SLOTS, 2, SUB, LAT), BF),
+            pltpu.VMEM((SLOTS, 2, SUB, LAT), BF),
+            pltpu.VMEM((SLOTS, SUB, LAT), BF),
             pltpu.VMEM((SLOTS, SUB, LAT), BF),
             pltpu.VMEM((SLOTS, SUB, LAT), BF),
             dma((2,)),
             dma((SLOTS,)), dma((SLOTS,)),
             dma((PARTS, HEADS)), dma((PARTS, HEADS)),
-            dma((3, 4)), dma((3, 4)),
-            dma((PAIRS, 3)), dma((PAIRS, 3)),
-            dma((PAIRS, 8)), dma((PAIRS, 8)),
+            dma((7,)), dma((7,)),
+            dma((PAIRS, 7)), dma((PAIRS, 7)),
+            dma((PAIRS, REACH)), dma((PAIRS, REACH)),
             dma((HEADS,)), dma((HEADS,)),
             dma((HEADS,)), dma((HEADS,)),
             dma((PARTS, HEADS)), dma((PARTS, HEADS)),
@@ -532,16 +608,34 @@
     )(x, kv, wq, wkv, do, trig, positions)
 
 
+def hand_over_kernel(*refs):
+    for source, target in zip(refs[:3], refs[3:]):
+        target[...] = source[...]
+
+
+def hand_over(*arrays):
+    vmem = pl.BlockSpec(memory_space=pltpu.VMEM)
+    return pl.pallas_call(
+        hand_over_kernel,
+        out_shape=tuple(jax.ShapeDtypeStruct(a.shape, a.dtype) for a in arrays),
+        in_specs=[vmem] * 3,
+        out_specs=(vmem,) * 3,
+        name="hand_over",
+    )(*arrays)
+
+
 def shards(query_latent, kv_latent, query_up, kv_up, out_grad, positions):
     s = lax.axis_index("seq")
     local_positions = lax.dynamic_slice_in_dim(positions[0], s * TOK, TOK)
     half = ROPE // 2
-    rates = 10000.0 ** (-jnp.arange(half, dtype=F32) / half)
+    lane = jnp.arange(ROPE)
+    rates = 10000.0 ** (-(lane % half).astype(F32) / half)
     angles = local_positions.astype(F32)[:, None] * rates[None, :]
-    trig = jnp.concatenate([jnp.cos(angles), jnp.sin(angles)], 1)
+    trig = jnp.where(lane[None, :] < half, jnp.cos(angles), jnp.sin(angles))
     query_grad, weight_grad, latent_grad = backward_pass(
-        query_latent[0], kv_latent[0], query_up, kv_up, out_grad[0], trig, positions
+        query_latent[0], kv_latent[0].T, query_up, kv_up, out_grad[0], trig, positions
     )
+    query_grad, weight_grad, latent_grad = hand_over(query_grad, weight_grad, latent_grad)
     return query_grad.reshape(1, TOK, QL), latent_grad[None], weight_grad
 
 

time: 116 us -> 107 us (0.922)
  local copies, waits for them, and re-layouts: 6.39 us -> 0 us
  Pallas kernels: 107 us -> 104 us
    unnamed x4 -> x0, local copies, waits for them, and re-layouts: 6.39 us -> none
    pallas_call x1, Pallas kernels: 107 us -> 103 us  [backward_pass(): pl.pallas_call(kernel, out_shape=(jax.ShapeDtypeStruct((HEADS, SUB, QL),...]
    pallas_call x0 -> x1, Pallas kernels: none -> 1.89 us  [hand_over(): pl.pallas_call(hand_over_kernel, out_shape=tuple((jax.ShapeDtypeStruct(a....]
where the time goes in v3:
time: 107 us
  Pallas kernels  104 us (97%)
  other arithmetic  1.62 us (2%)
    pallas_call x1, Pallas kernels, backward_pass(): pl.pallas_call(kernel, out_shape=(jax.ShapeDtypeStruct((HEADS, SUB, QL),...  103 us

profile of v3, /device:TPU:128, one launch (start us, length us, event | category | flops | bytes accessed | tf_op | source)
XLA Modules:
  0.0 106.7 jit_solution(18218654903004208631)
XLA Ops:
  0.6 0.7 convert_bitcast_fusion
  1.3 0.9 fusion.trig_ref
  2.3 102.6 %attention_backward.1 = (bf16[8,16,1536]{2,1,0:T(8,128)(2,1)}, bf16[48,1536]{1,0:T(8,128)(2,1)}, bf16[16,576]{1,0:T(8,128)(2,1)}) custom-call(bf16[128,1536]{1,0:T(8,128)(2,1)} %bitcast.9, bf16[576,128]{1,0:T(8,128)(2,1)} %bitcast.11, bf16[1536,1536]{1,0:T(8,128)(2,1)} %wq_hbm.1, bf16[512,2048]{1,0:T(8,128)(2,1)} %wkv_hbm.1, bf16[128,1024]{1,0:T(8,128)(2,1)} %bitcast.10, ...), custom_call_target="tpu_custom_call" | custom-call | tf_op jit(solution)/shard_map/attention_backward/pallas_call | solution.py:557
  104.8 1.9 %hand_over.1 = (bf16[8,16,1536]{2,1,0:T(8,128)(2,1)}, bf16[48,1536]{1,0:T(8,128)(2,1)}, bf16[16,576]{1,0:T(8,128)(2,1)}) custom-call(bf16[8,16,1536]{2,1,0:T(8,128)(2,1)} %get-tuple-element.9.refs_0_, bf16[48,1536]{1,0:T(8,128)(2,1)} %get-tuple-element.10.refs_1_, bf16[16,576]{1,0:T(8,128)(2,1)} %get-tuple-element.11.refs_2_), custom_call_target="tpu_custom_call" | custom-call | tf_op jit(solution)/shard_map/hand_over/pallas_call | solution.py:618
  (2 shorter events, 0.0 us)

commit v4 on v3

--- a/solution.py
+++ b/solution.py
@@ -91,7 +91,7 @@
     x_ref, kv_ref, wq_hbm, wkv_hbm, do_ref, trig_ref, pos_ref,
     qg_ref, w_ref, l_ref,
     wq_v, wkv_v, kvx_s, xt_s, lat_s, xg_s, a_s, r_s, kvd_s, sp_s, sr_s, dp_s, rope_s, acc_s,
-    dg_s, wp_s, rw_s, qt_s, rq_s, qs_s, dl_s, rl_s, ts_s, ry_s, ls_s, rlat_s,
+    dg_s, wp_s, rw_s, qt_s, rq_s, qs_s, dl_s, rl_s, ts_s, ry_s, rb_s, tb_s, rx_s, ls_s, rlat_s,
     load, s1, r1, s2, r2, sx, rx, sdq, rdq, sw, rw, sqt, rqt, sqa, rqa, sdl, rdl, sls, rls,
 ):
     r, s, h = place()
@@ -163,16 +163,46 @@
     def slots_of(p):
         return pl.ds(pl.multiple_of(4 * p, 4), 4)
 
-    def to_plane(p, d):
-        return remote(
-            lat_s.at[slots_of(p), h], lat_s.at[slots_of(p), h], s2.at[p, d], r2.at[p, d], (r, s, plane[d - 1])
-        )
-
-    def from_plane(p, d):
-        source = lax.rem(h - d + HEADS, HEADS)
-        return remote(
-            lat_s.at[slots_of(p), h], lat_s.at[slots_of(p), source], s2.at[p, d], r2.at[p, d], (r, s, source)
-        )
+    row, column = lax.div(h, 4), lax.rem(h, 4)
+
+    def early(p):
+        return pl.ds(pl.multiple_of(4 * p, 2), 2)
+
+    def late(p):
+        return pl.ds(pl.multiple_of(4 * p + 2, 2), 2)
+
+    def beside(d):
+        return lax.rem(column + d, 4)
+
+    def in_row(d):
+        return (r, s, 4 * row + beside(d))
+
+    opposite = (r, s, 4 * (1 - row) + column)
+
+    def behind(d):
+        return lax.rem(column - d + 4, 4)
+
+    def block(at, heads, to, p, n):
+        ref = lat_s.at[at, heads]
+        return remote(ref, ref, s2.at[p, n], r2.at[p, n], to)
+
+    turned_h = 4 * (1 - row) + column
+
+    def share_y(p, h_from=None):
+        return block(early(p), h if h_from is None else h_from, opposite, p, 0)
+
+    def share_x(p, d, h_from=None):
+        return block(early(p), h if h_from is None else h_from, in_row(d), p, d)
+
+    def share_yx(p, d, h_from=None):
+        return block(early(p), turned_h if h_from is None else h_from, in_row(d), p, 3 + d)
+
+    def late_x(p, d, h_from=None):
+        return block(late(p), h if h_from is None else h_from, in_row(d), p, 6 + d)
+
+    def late_xy(p, from_row=None):
+        at = pl.ds(pl.multiple_of(4 * (row if from_row is None else from_row), 4), 4)
+        return block(late(p), at, opposite, p, 10)
 
     scale = (NOPE + ROPE) ** (-0.5)
     cosine = jnp.concatenate([trig_ref[:, : ROPE // 2]] * 4, 1)
@@ -199,11 +229,28 @@
             @pl.when(older(4 * p + k))
             def _():
                 from_seq(4 * p + k).wait_recv()
-        for d in range(1, HEADS):
-            to_plane(p, d).start()
+        share_y(p).start()
+        for d in range(1, 4):
+            late_x(p, d).start()
+        for d in range(1, 4):
+            share_x(p, d).start()
+
+        @pl.when(i >= 1)
+        def _():
+            onward(p + 1)
+
         return nothing
 
+    def onward(p):
+        share_y(p, turned_h).wait_recv()
+        for d in range(1, 4):
+            share_yx(p, d).start()
+        for d in range(1, 4):
+            late_x(p, d, 4 * row + behind(d)).wait_recv()
+        late_xy(p).start()
+
     lax.fori_loop(0, parts, share, 0)
+    onward(0)
     turned = x_ref[...].T.reshape(2, 8, 2, 48, TOK)
     xt_s[:, :8] = turned
     xt_s[:, 8:] = turned
@@ -220,8 +267,10 @@
 
     def keys_of(i, nothing):
         p = part - i
-        for d in range(1, HEADS):
-            from_plane(p, d).wait_recv()
+        for d in range(1, 4):
+            share_x(p, d, 4 * row + behind(d)).wait_recv()
+            share_yx(p, d, 4 * (1 - row) + behind(d)).wait_recv()
+        late_xy(p, 1 - row).wait_recv()
         rows = latent_chunk(p)[:, :KVL]
         for g in range(PAIRS):
             kvd_s[g, chunk_at(p), :] = dot(rows, wkv_v[:, 512 * g : 512 * (g + 1)], NN).astype(BF)
@@ -385,35 +434,32 @@
 
     lax.fori_loop(0, PAIRS, pair, 0)
 
-    joined = jnp.concatenate([dg_s[g, mine] for g in range(PAIRS)], 1)
-    qt_s[...] = dot(joined, wq_v[...], NT).astype(BF).reshape(HEADS, SUB, QL)
-
     def query_out(d):
         return remote(qt_s.at[plane[d - 1]], rq_s.at[h], sqt.at[d], rqt.at[d], (r, s, plane[d - 1]))
 
-    for d in range(1, HEADS):
-        query_out(d).start()
-
-    row, column = lax.div(h, 4), lax.rem(h, 4)
-
-    def latent_out(p, d):
-        to = lax.rem(column + d, 4)
+    def send_queries():
+        joined = jnp.concatenate([dg_s[g, mine] for g in range(PAIRS)], 1)
+        qt_s[...] = dot(joined, wq_v[...], NT).astype(BF).reshape(HEADS, SUB, QL)
+        for d in range(1, HEADS):
+            query_out(d).start()
+
+
+    def latent_x(p, d, source=None):
+        at = column if source is None else source
         return remote(
-            dl_s.at[slots_of(p), :, to], rl_s.at[column, slots_of(p)], sdl.at[p, d], rdl.at[p, d],
-            (r, s, 4 * row + to),
+            dl_s.at[early(p), :, beside(d)], rl_s.at[at, early(p)], sdl.at[p, d], rdl.at[p, d], in_row(d)
         )
 
-    def latent_in(p, d):
-        source = lax.rem(column - d + 4, 4)
+    def latent_xy(p):
+        return remote(ts_s.at[early(p), 1 - row], ry_s.at[early(p)], sdl.at[p, 0], rdl.at[p, 0], opposite)
+
+    def latent_y(p):
+        return remote(dl_s.at[late(p), 1 - row], rb_s.at[late(p)], sdl.at[p, 4], rdl.at[p, 4], opposite)
+
+    def latent_yx(p, d, source=None):
+        at = column if source is None else source
         return remote(
-            dl_s.at[slots_of(p), :, column], rl_s.at[source, slots_of(p)], sdl.at[p, d], rdl.at[p, d],
-            (r, s, 4 * row + source),
-        )
-
-    def latent_cross(p):
-        return remote(
-            ts_s.at[slots_of(p), 1 - row], ry_s.at[slots_of(p)], sdl.at[p, 0], rdl.at[p, 0],
-            (r, s, 4 * (1 - row) + column),
+            tb_s.at[late(p), beside(d)], rx_s.at[at, late(p)], sdl.at[p, 4 + d], rdl.at[p, 4 + d], in_row(d)
         )
 
     def latents(p):
@@ -423,40 +469,24 @@
         rope = rope_s[at, :]
         rope = (rope + pltpu.roll(rope, ROPE, 1)).astype(BF)
         dl_s[slots_of(p)] = jnp.concatenate([low_part, rope], 1).reshape(4, 2, 4, SUB, LAT)
-        for d in range(1, 4):
-            latent_out(p, d).start()
-
-    latents(0)
-    relay_z(PAIRS - 1)
-    relay_zy(PAIRS - 2)
-
-    @pl.when(parts > 1)
-    def _():
-        latents(1)
-
-    relay_y(PAIRS - 1)
-    weights(PAIRS - 2)
-
-    @pl.when(parts > 2)
-    def _():
-        latents(2)
-
-    relay_zy(PAIRS - 1)
-    weights(PAIRS - 1)
-
-    total = qt_s[h].astype(F32)
-    for d in range(1, HEADS):
-        source = lax.rem(h - d + HEADS, HEADS)
-        remote(qt_s.at[h], rq_s.at[source], sqt.at[d], rqt.at[d], (r, s, source)).wait_recv()
-        total += rq_s[source].astype(F32)
-    qs_s[...] = total.astype(BF)
-    qg_ref[h] = qs_s[...]
+        latent_y(p).start()
+        for d in range(1, 4):
+            latent_x(p, d).start()
 
     def query_share(d):
         return remote(qs_s, qg_ref.at[h], sqa.at[d], rqa.at[d], (r, s, plane[d - 1]))
 
-    for d in range(1, HEADS):
-        query_share(d).start()
+    def share_queries():
+        total = qt_s[h].astype(F32)
+        for d in range(1, HEADS):
+            source = lax.rem(h - d + HEADS, HEADS)
+            remote(qt_s.at[h], rq_s.at[source], sqt.at[d], rqt.at[d], (r, s, source)).wait_recv()
+            total += rq_s[source].astype(F32)
+        qs_s[...] = total.astype(BF)
+        qg_ref[h] = qs_s[...]
+        for d in range(1, HEADS):
+            query_share(d).start()
+
 
     def to_latent_owner(k):
         return remote(ls_s.at[k], rlat_s.at[slot], sls.at[k], rls.at[slot], (r, base + k, h))
@@ -465,33 +495,54 @@
         return remote(ls_s.at[k], rlat_s.at[k], sls.at[k], rls.at[k], (r, base + k, h))
 
     def add_row(p):
-        for d in range(1, 4):
-            latent_in(p, d).wait_recv()
-        for k in range(4 * p, 4 * p + 4):
+        latent_y(p).wait_recv()
+        for k in (4 * p + 2, 4 * p + 3):
+            tb_s[k] = (dl_s[k, row].astype(F32) + rb_s[k].astype(F32)).astype(BF)
+        for d in range(1, 4):
+            latent_yx(p, d).start()
+        for d in range(1, 4):
+            latent_x(p, d, behind(d)).wait_recv()
+        for k in (4 * p, 4 * p + 1):
             total = dl_s[k, :, column].astype(F32)
             for d in range(1, 4):
-                total += rl_s[lax.rem(column + d, 4), k].astype(F32)
+                total += rl_s[beside(d), k].astype(F32)
             ts_s[k] = total.astype(BF)
-        latent_cross(p).start()
+        latent_xy(p).start()
 
     def add_column(p):
-        latent_cross(p).wait_recv()
+        for d in range(1, 4):
+            latent_yx(p, d, behind(d)).wait_recv()
+        latent_xy(p).wait_recv()
         for k in range(4 * p, 4 * p + 4):
-            ls_s[k] = (ts_s[k, row].astype(F32) + ry_s[k].astype(F32)).astype(BF)
+            if k % 4 < 2:
+                total = ts_s[k, row].astype(F32) + ry_s[k].astype(F32)
+            else:
+                total = tb_s[k, column].astype(F32)
+                for d in range(1, 4):
+                    total += rx_s[beside(d), k].astype(F32)
+            ls_s[k] = total.astype(BF)
 
             @pl.when(older(k))
             def _():
                 to_latent_owner(k).start()
 
+    latents(0)
+    relay_z(3)
+    relay_zy(2)
+    pl.when(parts > 1)(lambda: latents(1))
+    relay_y(3)
+    weights(2)
+    pl.when(parts > 2)(lambda: latents(2))
+    relay_zy(3)
+    weights(3)
+    send_queries()
     add_row(0)
-    for p in range(1, PARTS):
-        @pl.when(p < parts)
-        def _():
-            add_row(p)
-
-        add_column(p - 1) if p == 1 else pl.when(p - 1 < parts)(lambda: add_column(p - 1))
-
-    pl.when(PARTS - 1 < parts)(lambda: add_column(PARTS - 1))
+    pl.when(parts > 1)(lambda: add_row(1))
+    add_column(0)
+    share_queries()
+    pl.when(parts > 2)(lambda: add_row(2))
+    pl.when(parts > 1)(lambda: add_column(1))
+    pl.when(parts > 2)(lambda: add_column(2))
 
     for g in range(PAIRS):
         total = wp_s[g, piece(0)].astype(F32)
@@ -531,11 +582,17 @@
         columns(k).wait_send()
 
     def drain_part(p, nothing):
-        for d in range(1, HEADS):
-            to_plane(p, d).wait_send()
-        for d in range(1, 4):
-            latent_out(p, d).wait_send()
-        latent_cross(p).wait_send()
+        share_y(p).wait_send()
+        late_xy(p).wait_send()
+        for d in range(1, 4):
+            share_x(p, d).wait_send()
+            share_yx(p, d).wait_send()
+            late_x(p, d).wait_send()
+        for d in range(1, 4):
+            latent_x(p, d).wait_send()
+            latent_yx(p, d).wait_send()
+        latent_xy(p).wait_send()
+        latent_y(p).wait_send()
         return nothing
 
     lax.fori_loop(0, parts, drain_part, 0)
@@ -588,11 +645,14 @@
             pltpu.VMEM((4, SLOTS, 2, SUB, LAT), BF),
             pltpu.VMEM((SLOTS, 2, SUB, LAT), BF),
             pltpu.VMEM((SLOTS, SUB, LAT), BF),
+            pltpu.VMEM((SLOTS, 4, SUB, LAT), BF),
+            pltpu.VMEM((SLOTS, 4, SUB, LAT), BF),
+            pltpu.VMEM((4, SLOTS, SUB, LAT), BF),
             pltpu.VMEM((SLOTS, SUB, LAT), BF),
             pltpu.VMEM((SLOTS, SUB, LAT), BF),
             dma((2,)),
             dma((SLOTS,)), dma((SLOTS,)),
-            dma((PARTS, HEADS)), dma((PARTS, HEADS)),
+            dma((PARTS, 11)), dma((PARTS, 11)),
             dma((7,)), dma((7,)),
             dma((PAIRS, 7)), dma((PAIRS, 7)),
             dma((PAIRS, REACH)), dma((PAIRS, REACH)),

time: 107 us -> 99.9 us (0.934)
  Pallas kernels: 104 us -> 97.2 us
    pallas_call x1, Pallas kernels: 103 us -> 95.3 us  [backward_pass(): pl.pallas_call(kernel, out_shape=(jax.ShapeDtypeStruct((HEADS, SUB, QL),...]
where the time goes in v4:
time: 99.9 us; the launch traced here: 99.5 us
  Pallas kernels  97.2 us (97%)
  other arithmetic  1.62 us (2%)
    pallas_call x1, Pallas kernels, backward_pass(): pl.pallas_call(kernel, out_shape=(jax.ShapeDtypeStruct((HEADS, SUB, QL),...  95.3 us

profile of v4, /device:TPU:128, one launch (start us, length us, event | category | flops | bytes accessed | tf_op | source)
XLA Modules:
  0.0 99.5 jit_solution(11059706602885856727)
XLA Ops:
  0.6 0.7 convert_bitcast_fusion
  1.3 0.9 fusion.trig_ref
  2.3 95.3 %attention_backward.1 = (bf16[8,16,1536]{2,1,0:T(8,128)(2,1)}, bf16[48,1536]{1,0:T(8,128)(2,1)}, bf16[16,576]{1,0:T(8,128)(2,1)}) custom-call(bf16[128,1536]{1,0:T(8,128)(2,1)} %bitcast.9, bf16[576,128]{1,0:T(8,128)(2,1)} %bitcast.11, bf16[1536,1536]{1,0:T(8,128)(2,1)} %wq_hbm.1, bf16[512,2048]{1,0:T(8,128)(2,1)} %wkv_hbm.1, bf16[128,1024]{1,0:T(8,128)(2,1)} %bitcast.10, ...), custom_call_target="tpu_custom_call" | custom-call | tf_op jit(solution)/shard_map/attention_backward/pallas_call | solution.py:614
  97.6 1.9 %hand_over.1 = (bf16[8,16,1536]{2,1,0:T(8,128)(2,1)}, bf16[48,1536]{1,0:T(8,128)(2,1)}, bf16[16,576]{1,0:T(8,128)(2,1)}) custom-call(bf16[8,16,1536]{2,1,0:T(8,128)(2,1)} %get-tuple-element.9.refs_0_, bf16[48,1536]{1,0:T(8,128)(2,1)} %get-tuple-element.10.refs_1_, bf16[16,576]{1,0:T(8,128)(2,1)} %get-tuple-element.11.refs_2_), custom_call_target="tpu_custom_call" | custom-call | tf_op jit(solution)/shard_map/hand_over/pallas_call | solution.py:678
  (2 shorter events, 0.0 us)

commit v5 on v4

--- a/solution.py
+++ b/solution.py
@@ -530,18 +530,18 @@
     relay_z(3)
     relay_zy(2)
     pl.when(parts > 1)(lambda: latents(1))
+    pl.when(parts > 2)(lambda: latents(2))
     relay_y(3)
     weights(2)
-    pl.when(parts > 2)(lambda: latents(2))
+    add_row(0)
     relay_zy(3)
+    pl.when(parts > 1)(lambda: add_row(1))
     weights(3)
     send_queries()
-    add_row(0)
-    pl.when(parts > 1)(lambda: add_row(1))
     add_column(0)
-    share_queries()
     pl.when(parts > 2)(lambda: add_row(2))
     pl.when(parts > 1)(lambda: add_column(1))
+    share_queries()
     pl.when(parts > 2)(lambda: add_column(2))
 
     for g in range(PAIRS):

time: 99.9 us -> 95.7 us (0.958)
  Pallas kernels: 97.2 us -> 93.3 us
    pallas_call x1, Pallas kernels: 95.3 us -> 91.4 us  [backward_pass(): pl.pallas_call(kernel, out_shape=(jax.ShapeDtypeStruct((HEADS, SUB, QL),...]
where the time goes in v5:
time: 95.7 us; the launch traced here: 95.5 us
  Pallas kernels  93.3 us (97%)
  other arithmetic  1.62 us (2%)
    pallas_call x1, Pallas kernels, backward_pass(): pl.pallas_call(kernel, out_shape=(jax.ShapeDtypeStruct((HEADS, SUB, QL),...  91.4 us

profile of v5, /device:TPU:128, one launch (start us, length us, event | category | flops | bytes accessed | tf_op | source)
XLA Modules:
  0.0 95.5 jit_solution(17819411976520621627)
XLA Ops:
  0.6 0.7 convert_bitcast_fusion
  1.3 0.9 fusion.trig_ref
  2.3 91.4 %attention_backward.1 = (bf16[8,16,1536]{2,1,0:T(8,128)(2,1)}, bf16[48,1536]{1,0:T(8,128)(2,1)}, bf16[16,576]{1,0:T(8,128)(2,1)}) custom-call(bf16[128,1536]{1,0:T(8,128)(2,1)} %bitcast.9, bf16[576,128]{1,0:T(8,128)(2,1)} %bitcast.11, bf16[1536,1536]{1,0:T(8,128)(2,1)} %wq_hbm.1, bf16[512,2048]{1,0:T(8,128)(2,1)} %wkv_hbm.1, bf16[128,1024]{1,0:T(8,128)(2,1)} %bitcast.10, ...), custom_call_target="tpu_custom_call" | custom-call | tf_op jit(solution)/shard_map/attention_backward/pallas_call | solution.py:614
  93.7 1.9 %hand_over.1 = (bf16[8,16,1536]{2,1,0:T(8,128)(2,1)}, bf16[48,1536]{1,0:T(8,128)(2,1)}, bf16[16,576]{1,0:T(8,128)(2,1)}) custom-call(bf16[8,16,1536]{2,1,0:T(8,128)(2,1)} %get-tuple-element.9.refs_0_, bf16[48,1536]{1,0:T(8,128)(2,1)} %get-tuple-element.10.refs_1_, bf16[16,576]{1,0:T(8,128)(2,1)} %get-tuple-element.11.refs_2_), custom_call_target="tpu_custom_call" | custom-call | tf_op jit(solution)/shard_map/hand_over/pallas_call | solution.py:678
  (2 shorter events, 0.0 us)

commit v6 on v5

--- a/solution.py
+++ b/solution.py
@@ -528,17 +528,17 @@
 
     latents(0)
     relay_z(3)
+    pl.when(parts > 1)(lambda: latents(1))
     relay_zy(2)
-    pl.when(parts > 1)(lambda: latents(1))
     pl.when(parts > 2)(lambda: latents(2))
     relay_y(3)
     weights(2)
     add_row(0)
     relay_zy(3)
     pl.when(parts > 1)(lambda: add_row(1))
+    add_column(0)
     weights(3)
     send_queries()
-    add_column(0)
     pl.when(parts > 2)(lambda: add_row(2))
     pl.when(parts > 1)(lambda: add_column(1))
     share_queries()

time: 95.7 us -> 97.9 us (1.023)
  Pallas kernels: 93.3 us -> 94.9 us
    pallas_call x1, Pallas kernels: 91.4 us -> 93 us  [backward_pass(): pl.pallas_call(kernel, out_shape=(jax.ShapeDtypeStruct((HEADS, SUB, QL),...]
where the time goes in v6:
time: 97.9 us; the launch traced here: 97.2 us
  Pallas kernels  94.9 us (97%)
  other arithmetic  1.62 us (2%)
    pallas_call x1, Pallas kernels, backward_pass(): pl.pallas_call(kernel, out_shape=(jax.ShapeDtypeStruct((HEADS, SUB, QL),...  93 us

profile of v6, /device:TPU:128, one launch (start us, length us, event | category | flops | bytes accessed | tf_op | source)
XLA Modules:
  0.0 97.2 jit_solution(5308187307706181178)
XLA Ops:
  0.6 0.7 convert_bitcast_fusion
  1.3 0.9 fusion.trig_ref
  2.3 93.0 %attention_backward.1 = (bf16[8,16,1536]{2,1,0:T(8,128)(2,1)}, bf16[48,1536]{1,0:T(8,128)(2,1)}, bf16[16,576]{1,0:T(8,128)(2,1)}) custom-call(bf16[128,1536]{1,0:T(8,128)(2,1)} %bitcast.9, bf16[576,128]{1,0:T(8,128)(2,1)} %bitcast.11, bf16[1536,1536]{1,0:T(8,128)(2,1)} %wq_hbm.1, bf16[512,2048]{1,0:T(8,128)(2,1)} %wkv_hbm.1, bf16[128,1024]{1,0:T(8,128)(2,1)} %bitcast.10, ...), custom_call_target="tpu_custom_call" | custom-call | tf_op jit(solution)/shard_map/attention_backward/pallas_call | solution.py:614
  95.3 1.9 %hand_over.1 = (bf16[8,16,1536]{2,1,0:T(8,128)(2,1)}, bf16[48,1536]{1,0:T(8,128)(2,1)}, bf16[16,576]{1,0:T(8,128)(2,1)}) custom-call(bf16[8,16,1536]{2,1,0:T(8,128)(2,1)} %get-tuple-element.9.refs_0_, bf16[48,1536]{1,0:T(8,128)(2,1)} %get-tuple-element.10.refs_1_, bf16[16,576]{1,0:T(8,128)(2,1)} %get-tuple-element.11.refs_2_), custom_call_target="tpu_custom_call" | custom-call | tf_op jit(solution)/shard_map/hand_over/pallas_call | solution.py:678
  (2 shorter events, 0.0 us)
